TPU v7x, 256 devices: a whole 4x4x8 slice. The times are simulated.
256 devices in a mesh: tok: 32 (over z_hi, x, core), lyr: 8 (over z_lo, y).
Axes of the slice: x: 4, y: 4, z: 8 (z_hi: 4, z_lo: 2; z = z_hi * 2 + z_lo), core: 2. Of those that a mesh axis runs over, the one named last changes fastest.
Arguments:
- feature_codes: bfloat16 [16, 4096, 2, 256], P('lyr', 'tok'), may hold values from 0 to 21, as said below
- block_ids: int32 [16, 4096, 2], P('lyr', 'tok'), may hold values from 0 to 31, all different within a row; in each aligned block of 128 rows (0 to 127, 128 to 255, ..., all dimensions but the last counted through in order) at most 16 rows name the same one
- target_layer: int32 [4096], P('tok'), may hold values from 0 to 15
- request_ids: int32 [4096], P('tok'), may hold values from 0 to 15
- target_resid: bfloat16 [4096, 2304], P('tok'), may hold values from -6 to 6
- decoder: bfloat16 [16, 8192, 2304], P('lyr', 'tok'), may hold values from -0.25 to 0.25
Outputs:
- scores: bfloat16 [16, 4096, 2, 256], P('lyr', 'tok')
- request_totals: float32 [16, 16, 8192], P(None, 'lyr', 'tok')
Inputs may be any that keep to these rules, and one draw needn't show every extreme that they name: `block_ids`: the 2 panel indices of one token at one source layer are distinct; among the 128 tokens of one index of tok at one source layer no panel is named by more than 16 of them, a bound that some block reaches. `feature_codes`: nonnegative, with many entries zero.
All inputs are finite; a program needn't handle non-finite values.
Results may differ from a plain program's by a relative error of at most 0.0053.
Values may be sent and summed in bfloat16 or wider, within the bound.
No kernel may reach another device: no remote copies, remote signals or barrier semaphores. Data moves between devices by JAX's collectives and lax.ppermute only.
A program may use at most 64 MiB of HBM per device.

v0:
```python
import jax
import jax.numpy as jnp
from jax import lax
from jax.sharding import PartitionSpec as P

PANELS = 32
REQUESTS = 16
CAP = 16


def slot_of(flat_ids):
    one_hot = (flat_ids[:, None] == jnp.arange(PANELS, dtype=jnp.int32)[None, :]).astype(jnp.int32)
    before = jnp.cumsum(one_hot, axis=0) - one_hot
    return flat_ids * CAP + jnp.sum(before * one_hot, axis=1)


def source_of(slot_ids):
    row_count = slot_ids.shape[0]
    empty = jnp.full((PANELS * CAP,), row_count, jnp.int32)
    return empty.at[slot_ids].set(jnp.arange(row_count, dtype=jnp.int32))


def take_rows(table, index):
    return jnp.take(table, index, axis=0)


def pad_zero(table):
    return jnp.concatenate([table, jnp.zeros((1,) + table.shape[1:], table.dtype)], axis=0)


def normalize_error(resid_rows, rebuilt):
    error = resid_rows.astype(jnp.float32) - rebuilt
    spread = jnp.mean(error * error, axis=-1, keepdims=True)
    return (error * lax.rsqrt(spread + 1e-06)).astype(jnp.bfloat16)


def per_device(feature_codes, block_ids, target_layer, request_ids, target_resid, decoder):
    layers_here, count, kact, panel = feature_codes.shape
    width = target_resid.shape[1]
    tok_count = lax.axis_size("tok")
    per_dev = PANELS // tok_count
    rows_here = count * kact
    first_layer = lax.axis_index("lyr") * layers_here
    layer_ids = first_layer + jnp.arange(layers_here, dtype=jnp.int32)
    alive_mask = (layer_ids[:, None] <= target_layer[None, :]).astype(feature_codes.dtype)
    masked = feature_codes * alive_mask[:, :, None, None]
    flat_ids = block_ids.reshape(layers_here, rows_here)
    slot_ids = jax.vmap(slot_of)(flat_ids)
    source_rows = jax.vmap(source_of)(slot_ids)
    token_of = source_rows // kact
    code_rows = jax.vmap(pad_zero)(masked.reshape(layers_here, rows_here, panel))
    send_codes = jax.vmap(take_rows)(code_rows, source_rows).reshape(
        layers_here, tok_count, per_dev, CAP, panel
    )
    panel_weights = decoder.reshape(layers_here, per_dev, panel, width)
    received = lax.all_to_all(send_codes, "tok", split_axis=1, concat_axis=1, tiled=True)
    built = jnp.einsum(
        "lspcj,lpjd->lspcd", received, panel_weights, preferred_element_type=jnp.float32
    ).astype(jnp.bfloat16)
    returned = lax.all_to_all(built, "tok", split_axis=1, concat_axis=1, tiled=True).reshape(
        layers_here, PANELS * CAP, width
    )
    per_row = jax.vmap(take_rows)(returned, slot_ids)
    partial_value = jnp.sum(
        per_row.astype(jnp.float32).reshape(layers_here, count, kact, width), axis=(0, 2)
    )
    rebuilt = lax.psum(partial_value, "lyr")
    gradient = normalize_error(target_resid, rebuilt)
    send_grad = jnp.take(pad_zero(gradient), token_of, axis=0).reshape(
        layers_here, tok_count, per_dev, CAP, width
    )
    received_grad = lax.all_to_all(send_grad, "tok", split_axis=1, concat_axis=1, tiled=True)
    projected_slots = jnp.einsum(
        "lspcd,lpjd->lspcj", received_grad, panel_weights, preferred_element_type=jnp.float32
    ).astype(jnp.bfloat16)
    coming_back = lax.all_to_all(
        projected_slots, "tok", split_axis=1, concat_axis=1, tiled=True
    ).reshape(layers_here, PANELS * CAP, panel)
    picked = jax.vmap(take_rows)(coming_back, slot_ids).reshape(layers_here, count, kact, panel)
    attribution_rows = masked.astype(jnp.float32) * picked.astype(jnp.float32)
    scores = attribution_rows.astype(jnp.bfloat16)
    members = (request_ids[:, None] == jnp.arange(REQUESTS, dtype=jnp.int32)[None, :]).astype(
        jnp.float32
    )
    panel_hot = (block_ids[..., None] == jnp.arange(PANELS, dtype=jnp.int32)).astype(jnp.float32)
    local_totals = jnp.einsum(
        "tr,ltkn,ltkj->rlnj", members, panel_hot, attribution_rows, precision=lax.Precision.HIGHEST
    )
    local_totals = local_totals.reshape(REQUESTS, layers_here, PANELS * panel)
    request_totals = lax.psum_scatter(local_totals, "tok", scatter_dimension=2, tiled=True)
    return (scores, request_totals)


def solution(mesh):
    placed = (
        P("lyr", "tok", None, None),
        P("lyr", "tok", None),
        P("tok"),
        P("tok"),
        P("tok", None),
        P("lyr", "tok", None),
    )
    return jax.shard_map(
        per_device,
        mesh=mesh,
        in_specs=placed,
        out_specs=(P("lyr", "tok", None, None), P(None, "lyr", "tok")),
        check_vma=False,
    )
```

profile of v0, /device:TPU:1, one launch (start us, length us, event | category | flops | bytes accessed | tf_op | source)
XLA Modules:
  0.0 572.7 jit_solution(13679655794225082904)
XLA Ops:
  7.2 1.0 copy.77
  8.1 0.1 eq.52
  8.3 0.1 reshape.172
  8.4 0.7 broadcast_multiply_fusion.1
  9.1 1.2 reduce-window.6
  10.3 0.2 slice_reduce_fusion
  10.6 0.1 copy.82
  10.8 0.1 mul.57
  10.9 0.1 fusion.30
  11.0 24.5 %scatter_fusion = s32[2,512]{1,0:T(2,128)S(1)} fusion(s32[2,512]{1,0:T(2,128)S(1)} %broadcast_in_dim.67, s32[512]{0:T(512)S(1)} %bitcast.100, s32[512]{0:T(512)S(1)} %bitcast.109), kind=kCustom, calls=%fused_computation.4 | custom fusion | bytes 10240 | tf_op jit(solution)/shard_map/vmap()/scatter | solution.py:20
  35.7 0.3 broadcast_multiply_fusion
  36.1 0.4 copy.85
  36.6 0.2 concatenate.6
  36.8 10.3 %gather_fusion.1 = bf16[1024,256]{1,0:T(8,128)(2,1)} fusion(bf16[2,257,256]{2,0,1:T(2,128)(2,1)S(1)} %concatenate.6, s32[1024]{0:T(1024)S(1)} %bitcast.99), kind=kCustom, calls=%fused_computation.1 | custom fusion | bytes 1056768 | tf_op jit(solution)/shard_map/vmap(jit(_take))/gather | solution.py:24
  47.1 1.2 copy_select_fusion.1
  48.4 30.4 %all_to_all.20 = bf16[2,32,1,16,256]{4,3,0,2,1:T(8,128)(2,1)S(1)} all-to-all(bf16[2,32,1,16,256]{4,3,0,2,1:T(8,128)(2,1)S(1)} %copy_select_fusion.1), channel_id=1, replica_groups=mesh['tok'=32,'lyr'=8] {'tok'}, dimensions={1} | all-to-all | bytes 1048576 | tf_op jit(solution)/shard_map/all_to_all | solution.py:56
  78.8 1.4 fusion.2
  80.2 2.7 copy.88
  82.9 4.6 all-to-all-start.1
  87.5 0.2 all-reduce.4.cloned.1.call-start
  87.8 107.0 %all-to-all-done.1 = bf16[2,32,1,16,2304]{4,3,0,2,1:T(8,128)(2,1)} async-done(((bf16[2,32,1,16,2304]{4,3,0,2,1:T(8,128)(2,1)}), bf16[2,32,1,16,2304]{4,3,0,2,1:T(8,128)(2,1)}, u32[]{:S(2)}, u32[]{:S(2)}) %all-to-all-start.1) | async-done | bytes 4718624 | tf_op jit(solution)/shard_map/all_to_all | solution.py:60
  194.8 4.9 copy.89
  199.7 13.5 %gather_fusion.2 = bf16[512,2304]{1,0:T(8,128)(2,1)} fusion(bf16[2,512,2304]{2,1,0:T(8,128)(2,1)} %bitcast.98, s32[512]{0:T(512)S(1)} %bitcast.96), kind=kCustom, calls=%fused_computation.2 | custom fusion | bytes 4722688 | tf_op jit(solution)/shard_map/vmap(jit(_take))/gather | solution.py:24
  213.2 3.7 convert_reduce_fusion
  216.9 3.8 reduce_sum.42
  220.7 5.5 reduce_sum.43
  226.4 75.3 %all-reduce.4.cloned.1.call-done = f32[128,2304]{1,0:T(8,128)} async-done(((f32[128,2304]{1,0:T(8,128)}), f32[128,2304]{1,0:T(8,128)}) %all-reduce.4.cloned.1.call-update) | async-done | bytes 1179664 | tf_op jit(solution)/shard_map/psum | solution.py:67
  301.7 1.6 multiply_reduce_fusion
  303.4 0.2 multiply_convert_fusion
  303.6 6.2 %gather_fusion = bf16[1024,2304]{1,0:T(8,128)(2,1)} fusion(bf16[129,2304]{1,0:T(8,128)(2,1)S(1)} %concatenate.7, s32[1024]{0:T(1024)S(1)} %broadcast_clamp_fusion), kind=kCustom, calls=%fused_computation | custom fusion | bytes 9441280 | tf_op jit(solution)/shard_map/jit(_take)/gather | solution.py:69
  309.8 2.8 copy_select_fusion
  312.7 102.7 %all_to_all.21 = bf16[2,32,1,16,2304]{4,3,0,2,1:T(8,128)(2,1)S(1)} all-to-all(bf16[2,32,1,16,2304]{4,3,0,2,1:T(8,128)(2,1)S(1)} %copy_select_fusion), channel_id=1, replica_groups=mesh['tok'=32,'lyr'=8] {'tok'}, dimensions={1} | all-to-all | bytes 9437184 | tf_op jit(solution)/shard_map/all_to_all | solution.py:72
  415.4 1.4 fusion.16
  416.8 0.9 copy.93
  417.7 24.0 %all-to-all-start.3 = ((bf16[2,32,1,16,256]{4,3,0,2,1:T(8,128)(2,1)}), bf16[2,32,1,16,256]{4,3,0,2,1:T(8,128)(2,1)}, u32[]{:S(2)}, u32[]{:S(2)}) async-start(bf16[2,32,1,16,256]{4,3,0,2,1:T(8,128)(2,1)} %copy.93), calls=%async_computation.3 | async-start | bytes 1048576 | tf_op jit(solution)/shard_map/all_to_all | solution.py:76
  441.7 0.3 reduce-scatter.2.cloned.1.call-start
  441.9 0.1 reduce_sum.39
  442.2 0.2 copy.81
  442.4 16.2 %all-to-all-done.3 = bf16[2,32,1,16,256]{4,3,0,2,1:T(8,128)(2,1)} async-done(((bf16[2,32,1,16,256]{4,3,0,2,1:T(8,128)(2,1)}), bf16[2,32,1,16,256]{4,3,0,2,1:T(8,128)(2,1)}, u32[]{:S(2)}, u32[]{:S(2)}) %all-to-all-start.3) | async-done | bytes 524320 | tf_op jit(solution)/shard_map/all_to_all | solution.py:76
  458.6 1.1 copy.94
  459.6 5.6 gather_fusion.3
  465.2 1.1 gather.28
  466.3 5.6 fusion.23
  471.9 7.5 %fusion.8 = f32[2,32,2,8,256]{4,3,2,1,0:T(8,128)S(1)} fusion(f32[2,128,256,32]{2,3,1,0:T(8,128)S(1)} %fusion.23, s32[128]{0:T(128)S(1)} %copy-done.6), kind=kOutput, calls=%fused_computation.16 | convolution fusion | flops 402655232 | bytes 9437696 | tf_op jit(solution)/shard_map/tr,ltkn,ltkj->rlnj/dot_general | solution.py:86
  479.4 1.1 copy.103
  480.6 1.4 fusion.25
  481.9 82.6 %reduce-scatter.2.cloned.1.call-done = f32[16,2,256]{2,0,1:T(8,128)} async-done(((f32[16,2,8192]{2,0,1:T(8,128)}), f32[16,2,256]{2,0,1:T(8,128)}) %reduce-scatter.2.cloned.1.call-update) | async-done | bytes 32784 | tf_op jit(solution)/shard_map/reduce_scatter | solution.py:90
  564.5 1.4 copy.98
  (43 shorter events, 0.7 us)
Async XLA Ops:
  7.2 71.6 %copy-start = (bf16[2,256,2304]{2,1,0:T(8,128)(2,1)S(1)}, bf16[2,256,2304]{2,1,0:T(8,128)(2,1)}, u32[]{:S(2)}) copy-start(bf16[2,256,2304]{2,1,0:T(8,128)(2,1)} %param.11) | copy-start | bytes 7077892
  10.7 24.9 %copy-start.7 = (s32[128]{0:T(128)S(1)}, s32[128]{0:T(128)}, u32[]{:S(2)}) copy-start(s32[128]{0:T(128)} %param.8) | copy-start | bytes 1540
  10.7 25.0 %copy-start.3 = (bf16[2,128,2,256]{3,2,1,0:T(2,128)(2,1)S(1)}, bf16[2,128,2,256]{3,2,1,0:T(2,128)(2,1)}, u32[]{:S(2)}) copy-start(bf16[2,128,2,256]{3,2,1,0:T(2,128)(2,1)} %param.6) | copy-start | bytes 786436
  82.9 112.0 %all-to-all-start.1 = ((bf16[2,32,1,16,2304]{4,3,0,2,1:T(8,128)(2,1)}), bf16[2,32,1,16,2304]{4,3,0,2,1:T(8,128)(2,1)}, u32[]{:S(2)}, u32[]{:S(2)}) async-start(bf16[2,32,1,16,2304]{4,3,0,2,1:T(8,128)(2,1)} %copy.88), calls=%async_computation.1 | async-start | bytes 9437184 | tf_op jit(solution)/shard_map/all_to_all | solution.py:60
  87.5 214.2 %all-reduce.4.cloned.1.call-start = ((), (), s32[]{:S(2)}) async-start(), calls=%async_computation.5 | async-start | bytes 2359296 | tf_op jit(solution)/shard_map/psum | solution.py:67
  220.7 81.1 %copy-start.2 = (bf16[128,2304]{1,0:T(8,128)(2,1)S(1)}, bf16[128,2304]{1,0:T(8,128)(2,1)}, u32[]{:S(2)}) copy-start(bf16[128,2304]{1,0:T(8,128)(2,1)} %param.10) | copy-start | bytes 1769476
  301.7 1.6 copy-start.1
  416.8 25.4 %copy-start.5 = (s32[2,128,2]{1,2,0:T(2,128)S(1)}, s32[2,128,2]{1,2,0:T(2,128)}, u32[]{:S(2)}) copy-start(s32[2,128,2]{1,2,0:T(2,128)} %param.7) | copy-start | bytes 6148
  417.7 40.9 %all-to-all-start.3 = ((bf16[2,32,1,16,256]{4,3,0,2,1:T(8,128)(2,1)}), bf16[2,32,1,16,256]{4,3,0,2,1:T(8,128)(2,1)}, u32[]{:S(2)}, u32[]{:S(2)}) async-start(bf16[2,32,1,16,256]{4,3,0,2,1:T(8,128)(2,1)} %copy.93), calls=%async_computation.3 | async-start | bytes 1048576 | tf_op jit(solution)/shard_map/all_to_all | solution.py:76
  441.7 122.8 %reduce-scatter.2.cloned.1.call-start = ((), (), s32[]{:S(2)}) async-start(), calls=%async_computation.6 | async-start | bytes 1081344 | tf_op jit(solution)/shard_map/reduce_scatter | solution.py:90
  466.3 5.6 copy-start.6
  479.4 1.1 copy-start.4
Sparse Core Ops, SparseCore 0:
  226.4 75.3 all-reduce.3
  480.7 83.7 reduce-scatter.1
where the time goes:
time: 575 us; the launch traced here: 573 us
  waiting for transfers between devices  281 us (49%)
  blocking collectives  133 us (23%)
  local copies, waits for them, and re-layouts  80 us (14%)
  starting transfers between devices  29.1 us (5%)
  other arithmetic  19.1 us (3%)
  matrix products  15.9 us (3%)
  between operations  14.4 us (3%)
    all_to_all x1, waiting for transfers between devices, per_device(): lax.all_to_all(built, 'tok', split_axis=1, concat_axis=1, tiled=True)  107 us
    all_to_all x1, blocking collectives, per_device(): lax.all_to_all(send_grad, 'tok', split_axis=1, concat_axis=1, tiled=True)  103 us
    reduce_scatter x1, waiting for transfers between devices, per_device(): lax.psum_scatter(local_totals, 'tok', scatter_dimension=2, tiled=True)  82.6 us
    psum x1, waiting for transfers between devices, per_device(): rebuilt = lax.psum(partial_value, 'lyr')  75.3 us
    gather x4, local copies, waits for them, and re-layouts, take_rows(): return jnp.take(table, index, axis=0)  30.4 us
    all_to_all x1, blocking collectives, per_device(): lax.all_to_all(send_codes, 'tok', split_axis=1, concat_axis=1, tiled=True)  30.4 us
    scatter x1, local copies, waits for them, and re-layouts, source_of(): return empty.at[slot_ids].set(jnp.arange(row_count, dtype=jnp.int32))  24.5 us
    all_to_all x1, starting transfers between devices, per_device(): lax.all_to_all(projected_slots, 'tok', split_axis=1, concat_axis=1, tiled...  24 us
  transfers between devices with their start and end apart: 4, of which 4 were waited for; matrix products, arithmetic and copies ran while one was open for 0% of the time, Pallas kernels for 0%

commit v1 on v0

v1 whole, which is shorter than its diff:
```python
import jax
import jax.numpy as jnp
from jax import lax
from jax.experimental import pallas as pl
from jax.experimental.pallas import tpu as pltpu
from jax.sharding import Mesh, PartitionSpec as P

PANELS = 32
REQUESTS = 16
CAP = 16
LANES = 128
TOK = ("zh", "x", "c")
LYR = ("zl", "y")
PLANE = ("y", "x", "c")
COLUMN = ("zh", "zl")
EVERY = ("zh", "x", "c", "zl", "y")
BF16 = jnp.bfloat16
F32 = jnp.float32


def call(kernel, out_shape, flops, moved, scratch=(), limit=48):
    return pl.pallas_call(
        kernel,
        out_shape=out_shape,
        scratch_shapes=list(scratch),
        compiler_params=pltpu.CompilerParams(vmem_limit_bytes=limit * 1024 * 1024),
        cost_estimate=pl.CostEstimate(flops=flops, bytes_accessed=moved, transcendentals=0),
    )


def iota(shape, axis):
    return lax.broadcasted_iota(jnp.int32, shape, axis)


def to_column(row):
    n = row.shape[1]
    diag = iota((n, n), 0) == iota((n, n), 1)
    return jnp.sum(jnp.where(diag, jnp.broadcast_to(row, (n, n)), jnp.zeros((n, n), row.dtype)), axis=1, keepdims=True)


def pack_kernel(layer_ref, ids_ref, target_ref, request_ref, codes_ref, out_ref, slot_ref):
    layers, rows = ids_ref.shape
    tokens = target_ref.shape[1]
    request = request_ref[...].astype(F32)
    request_col = to_column(jnp.concatenate([request, request], axis=1))
    token_col = (iota((rows, 1), 0) % tokens + 1).astype(F32)
    lane = iota((rows, LANES), 1)
    extra = jnp.where(lane == 0, token_col, jnp.where(lane == 1, request_col, 0.0)).astype(BF16)
    target = target_ref[...]
    target_row = jnp.concatenate([target, target], axis=1)
    for l in range(layers):
        ids_row = ids_ref[l : l + 1, :].astype(F32)
        ids_col = to_column(ids_row)
        earlier = (ids_col == ids_row) & (iota((rows, rows), 0) < iota((rows, rows), 1))
        rank = jnp.sum(jnp.where(earlier, 1.0, 0.0), axis=0, keepdims=True)
        slot = (ids_row * CAP + rank).astype(jnp.int32)
        slot = jnp.where(target_row >= layer_ref[0] + l, slot, -1)
        slot_ref[l : l + 1, :] = slot
        pick = jnp.where(iota((PANELS * CAP, rows), 0) == slot, 1.0, 0.0).astype(BF16)
        panel = codes_ref.shape[2]
        sent = jnp.dot(pick, codes_ref[l], preferred_element_type=F32).astype(BF16)
        out_ref[:, l * CAP : (l + 1) * CAP, 0:panel] = sent.reshape(PANELS, CAP, panel)
        info = jnp.dot(pick, extra, preferred_element_type=F32).astype(BF16)
        out_ref[:, l * CAP : (l + 1) * CAP, panel : panel + LANES] = info.reshape(PANELS, CAP, LANES)


def build_kernel(codes_ref, weight_ref, out_ref):
    blocks, slots, _ = codes_ref.shape
    layers, panel, width = weight_ref.shape
    step = 256

    def body(n, carry):
        cols = pl.ds(pl.multiple_of(n * step, step), step)
        for l in range(layers):
            codes = codes_ref[:, l * CAP : (l + 1) * CAP, 0:panel].reshape(blocks * CAP, panel)
            built = jnp.dot(codes, weight_ref[l, :, cols], preferred_element_type=F32).astype(BF16)
            out_ref[:, l * CAP : (l + 1) * CAP, cols] = built.reshape(blocks, CAP, step)
        return carry

    lax.fori_loop(0, width // step, body, 0)
    out_ref[:, :, width : width + LANES] = codes_ref[:, :, panel : panel + LANES]


def reduce_kernel(rows_ref, out_ref, hot_ref):
    groups, slots, wide = rows_ref.shape
    width = wide - LANES
    tokens = hot_ref.shape[1]
    count = groups * slots
    step = 256
    token = rows_ref[:, :, width : width + LANES].reshape(count, LANES).astype(F32)[:, 0:1]
    hot = jnp.where(token == (iota((count, tokens), 1) + 1).astype(F32), 1.0, 0.0)
    hot_ref[...] = hot.astype(BF16)
    hot_t = hot.T.astype(BF16)

    def body(n, carry):
        cols = pl.ds(pl.multiple_of(n * step, step), step)
        rows = rows_ref[:, :, cols].reshape(count, step)
        out_ref[:, cols] = jnp.dot(hot_t, rows, preferred_element_type=F32).astype(out_ref.dtype)
        return carry

    lax.fori_loop(0, width // step, body, 0)


def gradient_kernel(parts_ref, resid_ref, out_ref):
    planes, tokens, width = parts_ref.shape
    rebuilt = parts_ref[0].astype(F32)
    for i in range(1, planes):
        rebuilt = rebuilt + parts_ref[i].astype(F32)
    error = resid_ref[...].astype(F32) - rebuilt
    spread = jnp.sum(error * error, axis=-1, keepdims=True) * (1.0 / width)
    gradient = (error * lax.rsqrt(spread + 1e-06)).astype(BF16)
    for i in range(planes):
        out_ref[i] = gradient


def spread_kernel(hot_ref, gradient_ref, out_ref):
    groups, slots, width = out_ref.shape
    step = 256

    def body(n, carry):
        cols = pl.ds(pl.multiple_of(n * step, step), step)
        rows = jnp.dot(hot_ref[...], gradient_ref[:, cols], preferred_element_type=F32).astype(BF16)
        out_ref[:, :, cols] = rows.reshape(groups, slots, step)
        return carry

    lax.fori_loop(0, width // step, body, 0)


def project_kernel(rows_ref, codes_ref, weight_ref, score_ref, total_ref):
    blocks, slots, width = rows_ref.shape
    layers, panel, _ = weight_ref.shape
    part = 8
    total_ref[...] = jnp.zeros_like(total_ref)

    def body(m, carry):
        here = pl.ds(m * part, part)
        for l in range(layers):
            inside = slice(l * CAP, (l + 1) * CAP)
            rows = rows_ref[here, inside, :].reshape(part * CAP, width)
            projected = lax.dot_general(
                rows, weight_ref[l], (((1,), (1,)), ((), ())), preferred_element_type=F32
            ).astype(BF16)
            codes = codes_ref[here, inside, 0:panel].reshape(part * CAP, panel).astype(F32)
            request = codes_ref[here, inside, panel : panel + LANES].reshape(part * CAP, LANES).astype(F32)[:, 1:2]
            value = codes * projected.astype(F32)
            score_ref[here, inside, :] = value.astype(BF16).reshape(part, CAP, panel)
            member = jnp.where(request == iota((part * CAP, LANES), 1).astype(F32), 1.0, 0.0)
            summed = jnp.dot(member.T, value, precision=lax.Precision.HIGHEST, preferred_element_type=F32)
            total_ref[l] = total_ref[l] + summed[0:REQUESTS]
        return carry

    lax.fori_loop(0, blocks // part, body, 0)


def place_kernel(slot_ref, scores_ref, out_ref):
    layers, rows = slot_ref.shape
    panel = scores_ref.shape[2]
    for l in range(layers):
        pick_t = jnp.where(iota((PANELS * CAP, rows), 0) == slot_ref[l : l + 1, :], 1.0, 0.0)
        pick = pick_t.T.astype(BF16)
        scores = scores_ref[:, l * CAP : (l + 1) * CAP, :].reshape(PANELS * CAP, panel)
        out_ref[l] = jnp.dot(pick, scores, preferred_element_type=F32).astype(BF16)


def per_device(feature_codes, block_ids, target_layer, request_ids, target_resid, decoder):
    layers, count, kact, panel = feature_codes.shape
    width = target_resid.shape[1]
    rows = count * kact
    blocks = lax.axis_size(TOK)
    planes = lax.axis_size(COLUMN)
    share = count // planes
    slots = layers * CAP
    zh, zl, y = lax.axis_index("zh"), lax.axis_index("zl"), lax.axis_index("y")
    first_layer = lax.axis_index(LYR) * layers

    sizes = [lax.axis_size(a) for a in EVERY]
    swap = []
    for d in range(sizes[0] * sizes[1] * sizes[2] * sizes[3] * sizes[4]):
        rest, d_y = divmod(d, sizes[4])
        rest, d_zl = divmod(rest, sizes[3])
        d_zh, d_xc = divmod(rest, sizes[1] * sizes[2])
        swap.append((d, ((d_y * sizes[1] * sizes[2] + d_xc) * sizes[3] + d_zl) * sizes[4] + d_zh))
    mine = lax.dynamic_slice_in_dim(target_resid, (y * sizes[3] + zl) * share, share, 0)
    resid = lax.ppermute(mine, EVERY, swap)

    ids = block_ids.transpose(0, 2, 1).reshape(layers, rows)
    codes = feature_codes.transpose(0, 2, 1, 3).reshape(layers, rows, panel)
    layer_arr = first_layer.reshape(1).astype(jnp.int32)
    sent, slot = pl.pallas_call(
        pack_kernel,
        out_shape=(
            jax.ShapeDtypeStruct((blocks, slots, panel + LANES), BF16),
            jax.ShapeDtypeStruct((layers, rows), jnp.int32),
        ),
        in_specs=[pl.BlockSpec(memory_space=pltpu.SMEM)] + [pl.BlockSpec(memory_space=pltpu.VMEM)] * 4,
        compiler_params=pltpu.CompilerParams(vmem_limit_bytes=32 * 1024 * 1024),
        cost_estimate=pl.CostEstimate(flops=300_000_000, bytes_accessed=1_000_000, transcendentals=0),
    )(layer_arr, ids, target_layer.reshape(1, count), request_ids.reshape(1, count), codes)
    codes_in = lax.all_to_all(sent, TOK, 0, 0, tiled=True)

    built = call(
        build_kernel, jax.ShapeDtypeStruct((blocks, slots, width + LANES), BF16), 1_200_000_000, 8_000_000
    )(codes_in, decoder)
    rows_in = lax.all_to_all(built, PLANE, 0, 0, tiled=True)
    partial, hot = call(
        reduce_kernel,
        (jax.ShapeDtypeStruct((count, width), BF16), jax.ShapeDtypeStruct((blocks * slots, count), BF16)),
        600_000_000,
        6_000_000,
    )(rows_in)
    parts = lax.all_to_all(partial.reshape(planes, share, width), COLUMN, 0, 0, tiled=True)
    copies = call(gradient_kernel, jax.ShapeDtypeStruct((planes, share, width), BF16), 1_000_000, 1_200_000)(
        parts, resid
    )
    gradient = lax.all_to_all(copies, COLUMN, 0, 0, tiled=True).reshape(count, width)
    spread = call(spread_kernel, jax.ShapeDtypeStruct((blocks, slots, width), BF16), 600_000_000, 6_000_000)(
        hot, gradient
    )
    grad_in = lax.all_to_all(spread, PLANE, 0, 0, tiled=True)
    scored, totals = call(
        project_kernel,
        (
            jax.ShapeDtypeStruct((blocks, slots, panel), BF16),
            jax.ShapeDtypeStruct((layers, REQUESTS, panel), F32),
        ),
        1_300_000_000,
        8_000_000,
    )(grad_in, codes_in, decoder)
    scores_in = lax.all_to_all(scored, TOK, 0, 0, tiled=True)
    placed = call(place_kernel, jax.ShapeDtypeStruct((layers, rows, panel), BF16), 140_000_000, 1_000_000)(
        slot, scores_in
    )
    scores = placed.reshape(layers, kact, count, panel).transpose(0, 2, 1, 3)
    return scores, totals.transpose(1, 0, 2)


def solution(mesh):
    fine = Mesh(mesh.devices.reshape(4, 4, 2, 2, 4), EVERY)
    placed = (
        P(LYR, TOK, None, None),
        P(LYR, TOK, None),
        P(TOK),
        P(TOK),
        P(TOK, None),
        P(LYR, TOK, None),
    )
    return jax.shard_map(
        per_device,
        mesh=fine,
        in_specs=placed,
        out_specs=(P(LYR, TOK, None, None), P(None, LYR, TOK)),
        check_vma=False,
    )
```

time: 575 us -> 267 us (0.46)
  waiting for transfers between devices: 281 us -> 35.8 us
  local copies, waits for them, and re-layouts: 80 us -> 9.68 us
  blocking collectives: 133 us -> 190 us
  Pallas kernels: 0 us -> 22.1 us
  starting transfers between devices: 29.1 us -> 8.19 us
  other arithmetic: 19.1 us -> 0 us
  matrix products: 15.9 us -> 0 us
  between operations: 14.4 us -> 0.8 us
    all_to_all x2, waiting for transfers between devices: 123 us -> 35.8 us  [the longest x1 17.9 us: per_device(): lax.all_to_all(partial.reshape(planes, share, width), COLUMN, 0, 0, tiled...]
    reduce_scatter x1 -> x0, waiting for transfers between devices: 82.6 us -> none  [per_device(): lax.psum_scatter(local_totals, 'tok', scatter_dimension=2, tiled=True)]
    psum x1 -> x0, waiting for transfers between devices: 75.3 us -> none  [per_device(): rebuilt = lax.psum(partial_value, 'lyr')]
    all_to_all x2 -> x4, blocking collectives: 133 us -> 190 us  [the longest x1 67.1 us: per_device(): rows_in = lax.all_to_all(built, PLANE, 0, 0, tiled=True)]
    gather x5 -> x0, local copies, waits for them, and re-layouts: 36.6 us -> none  [the longest x4 30.4 us: take_rows(): return jnp.take(table, index, axis=0)]
    scatter x1 -> x0, local copies, waits for them, and re-layouts: 24.5 us -> none  [source_of(): return empty.at[slot_ids].set(jnp.arange(row_count, dtype=jnp.int32))]
    pallas_call x0 -> x7, Pallas kernels: none -> 22.1 us  [the longest x1 11.1 us: per_device(): call(project_kernel, (jax.ShapeDtypeStruct((blocks, slots, panel), BF16),...]
    all_to_all x2, starting transfers between devices: 28.6 us -> 7.52 us  [the longest x1 3.99 us: per_device(): scores_in = lax.all_to_all(scored, TOK, 0, 0, tiled=True)]
  transfers between devices with their start and end apart: 4 -> 3, of which waited for: 4 -> 2; matrix products, arithmetic and copies ran while one was open for 0% -> 0% of each run, Pallas kernels for 0% -> 0%
where the time goes in v1:
time: 267 us; the launch traced here: 266 us
  blocking collectives  190 us (71%)
  waiting for transfers between devices  35.8 us (13%)
  Pallas kernels  22.1 us (8%)
  local copies, waits for them, and re-layouts  9.68 us (4%)
  starting transfers between devices  8.19 us (3%)
    all_to_all x1, blocking collectives, per_device(): rows_in = lax.all_to_all(built, PLANE, 0, 0, tiled=True)  67.1 us
    all_to_all x1, blocking collectives, per_device(): grad_in = lax.all_to_all(spread, PLANE, 0, 0, tiled=True)  65 us
    all_to_all x1, blocking collectives, per_device(): codes_in = lax.all_to_all(sent, TOK, 0, 0, tiled=True)  34.9 us
    all_to_all x1, blocking collectives, per_device(): lax.all_to_all(copies, COLUMN, 0, 0, tiled=True).reshape(count, width)  22.8 us
    all_to_all x1, waiting for transfers between devices, per_device(): lax.all_to_all(partial.reshape(planes, share, width), COLUMN, 0, 0, tiled...  17.9 us
    all_to_all x1, waiting for transfers between devices, per_device(): scores_in = lax.all_to_all(scored, TOK, 0, 0, tiled=True)  17.8 us
    pallas_call x1, Pallas kernels, per_device(): call(project_kernel, (jax.ShapeDtypeStruct((blocks, slots, panel), BF16),...  11.1 us
    unnamed x24, local copies, waits for them, and re-layouts  7.68 us
  transfers between devices with their start and end apart: 3, of which 2 were waited for; matrix products, arithmetic and copies ran while one was open for 0% of the time, Pallas kernels for 0%

profile of v1, /device:TPU:1, one launch (start us, length us, event | category | flops | bytes accessed | tf_op | source)
XLA Modules:
  0.0 266.3 jit_solution(16026765564832240192)
XLA Ops:
  0.6 0.0 copy-start
  0.6 0.0 copy-start.1
  0.7 0.8 copy.15
  1.5 1.0 copy.8
  2.5 0.0 copy-start.9
  2.5 0.6 copy-done.9
  3.2 0.0 copy-start.10
  3.2 0.7 copy-done.10
  3.8 0.6 shard_map.77
  4.4 34.9 %all_to_all.30.codes_ref = bf16[32,32,384]{2,1,0:T(8,128)(2,1)S(1)} all-to-all(bf16[32,32,384]{2,1,0:T(8,128)(2,1)S(1)} %get-tuple-element.9), channel_id=1, replica_groups=mesh['zh'=4,'x'=4,'c'=2,'zl'=2,'y'=4] {'zh','x','c'}, dimensions={0} | all-to-all | bytes 1572864 | tf_op jit(solution)/shard_map/all_to_all | solution.py:199
  39.3 0.0 copy-done.1
  39.3 4.9 %shard_map.78 = bf16[32,32,2432]{2,1,0:T(8,128)(2,1)} custom-call(bf16[32,32,384]{2,1,0:T(8,128)(2,1)S(1)} %all_to_all.30.codes_ref, bf16[2,256,2304]{2,1,0:T(8,128)(2,1)S(1)} %copy-done.1), custom_call_target="tpu_custom_call" | custom-call | flops 1200000000 | bytes 8000000 | tf_op jit(solution)/shard_map/pallas_call | solution.py:201
  44.3 0.0 copy-start.2
  44.3 0.9 copy-done.2
  45.2 67.1 %all_to_all.31.rows_ref = bf16[32,32,2432]{2,1,0:T(8,128)(2,1)S(1)} all-to-all(bf16[32,32,2432]{2,1,0:T(8,128)(2,1)} %shard_map.78), channel_id=1, replica_groups=mesh['zh'=4,'x'=4,'c'=2,'zl'=2,'y'=4] {'y','x','c'}, dimensions={0} | all-to-all | bytes 9961472 | tf_op jit(solution)/shard_map/all_to_all | solution.py:204
  112.3 2.4 shard_map.79
  114.6 0.0 copy-start.4
  114.7 0.8 copy-done.4
  115.5 0.0 copy-start.5
  115.5 0.7 copy-done.5
  116.2 3.5 %all-to-all-start.2 = ((bf16[8,16,2304]{2,1,0:T(8,128)(2,1)}), bf16[8,16,2304]{2,1,0:T(8,128)(2,1)S(1)}, u32[]{:S(2)}, u32[]{:S(2)}) async-start(bf16[8,16,2304]{2,1,0:T(8,128)(2,1)} %bitcast.19), calls=%async_computation.2 | async-start | bytes 1179648 | tf_op jit(solution)/shard_map/all_to_all | solution.py:211
  119.7 0.0 copy-done
  119.8 0.7 collective-permute-start
  120.4 0.0 collective-permute-done.resid_ref
  120.4 0.0 copy-start.7
  120.5 0.6 copy-done.7
  121.1 17.9 %all-to-all-done.2.parts_ref = bf16[8,16,2304]{2,1,0:T(8,128)(2,1)S(1)} async-done(((bf16[8,16,2304]{2,1,0:T(8,128)(2,1)}), bf16[8,16,2304]{2,1,0:T(8,128)(2,1)S(1)}, u32[]{:S(2)}, u32[]{:S(2)}) %all-to-all-start.2) | async-done | bytes 589856 | tf_op jit(solution)/shard_map/all_to_all | solution.py:211
  139.0 0.0 copy-start.8
  139.0 0.9 copy-done.8
  139.9 0.2 shard_map.80
  140.1 22.8 %all_to_all.32 = bf16[8,16,2304]{2,1,0:T(8,128)(2,1)S(1)} all-to-all(bf16[8,16,2304]{2,1,0:T(8,128)(2,1)S(1)} %shard_map.80), channel_id=1, replica_groups=mesh['zh'=4,'x'=4,'c'=2,'zl'=2,'y'=4] {'zh','zl'}, dimensions={0} | all-to-all | bytes 1179648 | tf_op jit(solution)/shard_map/all_to_all | solution.py:215
  162.9 0.0 copy-start.6
  162.9 0.9 copy-done.6
  163.8 2.6 shard_map.81
  166.4 0.0 copy-start.3
  166.4 65.0 %all_to_all.33.rows_ref = bf16[32,32,2304]{2,1,0:T(8,128)(2,1)} all-to-all(bf16[32,32,2304]{2,1,0:T(8,128)(2,1)S(1)} %shard_map.81), channel_id=1, replica_groups=mesh['zh'=4,'x'=4,'c'=2,'zl'=2,'y'=4] {'y','x','c'}, dimensions={0} | all-to-all | bytes 9437184 | tf_op jit(solution)/shard_map/all_to_all | solution.py:219
  231.4 0.0 copy-done.3
  231.4 11.1 %shard_map.82 = (bf16[32,32,256]{2,1,0:T(8,128)(2,1)}, f32[2,16,256]{2,1,0:T(8,128)S(1)}) custom-call(bf16[32,32,2304]{2,1,0:T(8,128)(2,1)} %all_to_all.33.rows_ref, bf16[32,32,384]{2,1,0:T(8,128)(2,1)S(1)} %copy-done.3, bf16[2,256,2304]{2,1,0:T(8,128)(2,1)S(1)} %copy-done.1), custom_call_target="tpu_custom_call" | custom-call | flops 1300000000 | bytes 8000000 | tf_op jit(solution)/shard_map/pallas_call | solution.py:220
  242.5 4.0 %all-to-all-start.5 = ((bf16[32,32,256]{2,1,0:T(8,128)(2,1)}), bf16[32,32,256]{2,1,0:T(8,128)(2,1)S(1)}, u32[]{:S(2)}, u32[]{:S(2)}) async-start(bf16[32,32,256]{2,1,0:T(8,128)(2,1)} %get-tuple-element.12), calls=%async_computation.5 | async-start | bytes 1048576 | tf_op jit(solution)/shard_map/all_to_all | solution.py:229
  246.5 0.6 copy.10
  247.1 17.8 %all-to-all-done.5.scores_ref = bf16[32,32,256]{2,1,0:T(8,128)(2,1)S(1)} async-done(((bf16[32,32,256]{2,1,0:T(8,128)(2,1)}), bf16[32,32,256]{2,1,0:T(8,128)(2,1)S(1)}, u32[]{:S(2)}, u32[]{:S(2)}) %all-to-all-start.5) | async-done | bytes 524320 | tf_op jit(solution)/shard_map/all_to_all | solution.py:229
  265.0 0.4 shard_map.83
  265.3 1.0 copy.14
  (1 shorter events, 0.0 us)
Async XLA Ops:
  0.6 119.1 %copy-start = (bf16[128,2304]{1,0:T(8,128)(2,1)S(1)}, bf16[128,2304]{1,0:T(8,128)(2,1)}, u32[]{:S(2)}) copy-start(bf16[128,2304]{1,0:T(8,128)(2,1)} %param.10) | copy-start | bytes 1769476
  0.6 38.7 %copy-start.1 = (bf16[2,256,2304]{2,1,0:T(8,128)(2,1)S(1)}, bf16[2,256,2304]{2,1,0:T(8,128)(2,1)}, u32[]{:S(2)}) copy-start(bf16[2,256,2304]{2,1,0:T(8,128)(2,1)} %weight_ref.3) | copy-start | bytes 7077892
  2.5 0.7 copy-start.9
  3.2 0.7 copy-start.10
  44.3 0.9 copy-start.2
  114.6 0.8 copy-start.4
  115.5 0.7 copy-start.5
  116.2 22.8 %all-to-all-start.2 = ((bf16[8,16,2304]{2,1,0:T(8,128)(2,1)}), bf16[8,16,2304]{2,1,0:T(8,128)(2,1)S(1)}, u32[]{:S(2)}, u32[]{:S(2)}) async-start(bf16[8,16,2304]{2,1,0:T(8,128)(2,1)} %bitcast.19), calls=%async_computation.2 | async-start | bytes 1179648 | tf_op jit(solution)/shard_map/all_to_all | solution.py:211
  119.8 0.7 collective-permute-start
  120.4 0.6 copy-start.7
  139.0 0.9 copy-start.8
  162.9 1.0 copy-start.6
  166.4 65.0 %copy-start.3 = (bf16[32,32,384]{2,1,0:T(8,128)(2,1)S(1)}, bf16[32,32,384]{2,1,0:T(8,128)(2,1)}, u32[]{:S(2)}) copy-start(bf16[32,32,384]{2,1,0:T(8,128)(2,1)} %copy-done.2) | copy-start | bytes 2359300
  242.5 22.5 %all-to-all-start.5 = ((bf16[32,32,256]{2,1,0:T(8,128)(2,1)}), bf16[32,32,256]{2,1,0:T(8,128)(2,1)S(1)}, u32[]{:S(2)}, u32[]{:S(2)}) async-start(bf16[32,32,256]{2,1,0:T(8,128)(2,1)} %get-tuple-element.12), calls=%async_computation.5 | async-start | bytes 1048576 | tf_op jit(solution)/shard_map/all_to_all | solution.py:229

commit v2 on v1

v2 whole, which is shorter than its diff:
```python
import jax
import jax.numpy as jnp
from jax import lax
from jax.experimental import pallas as pl
from jax.experimental.pallas import tpu as pltpu
from jax.sharding import Mesh, PartitionSpec as P

PANELS = 32
REQUESTS = 16
CAP = 16
LANES = 128
TOK = ("zh", "x", "c")
LYR = ("zl", "y")
PLANE = ("y", "x", "c")
COLUMN = ("zh", "zl")
EVERY = ("zh", "x", "c", "zl", "y")
BF16 = jnp.bfloat16
F32 = jnp.float32


def call(kernel, out_shape, flops, moved, scratch=(), limit=20):
    return pl.pallas_call(
        kernel,
        out_shape=out_shape,
        scratch_shapes=list(scratch),
        compiler_params=pltpu.CompilerParams(vmem_limit_bytes=limit * 1024 * 1024),
        cost_estimate=pl.CostEstimate(flops=flops, bytes_accessed=moved, transcendentals=0),
    )


def iota(shape, axis):
    return lax.broadcasted_iota(jnp.int32, shape, axis)


def to_column(row):
    n = row.shape[1]
    diag = iota((n, n), 0) == iota((n, n), 1)
    return jnp.sum(jnp.where(diag, jnp.broadcast_to(row, (n, n)), jnp.zeros((n, n), row.dtype)), axis=1, keepdims=True)


def lane_groups(info):
    groups = info.shape[0]
    return jnp.sum(info.reshape(groups // 4, 4, 1, LANES), axis=1)


def pack_kernel(where_ref, ids_ref, target_ref, request_ref, codes_ref, out_ref, slot_ref):
    layers, rows = ids_ref.shape
    tokens = target_ref.shape[1]
    panel = codes_ref.shape[2]
    slots = layers * CAP
    per = LANES // slots
    halves = panel // LANES
    target = target_ref[...]
    target_row = jnp.concatenate([target, target], axis=1)
    request = request_ref[...].astype(F32) + 1.0
    request_row = jnp.concatenate([request, request], axis=1)
    token_row = (iota((1, rows), 1) % tokens + 1).astype(F32)
    token_info = jnp.zeros((PANELS, LANES), F32)
    request_info = jnp.zeros((PANELS, LANES), F32)
    for l in range(layers):
        ids_row = ids_ref[l : l + 1, :].astype(F32)
        ids_col = to_column(ids_row)
        earlier = (ids_col == ids_row) & (iota((rows, rows), 0) < iota((rows, rows), 1))
        rank = jnp.sum(jnp.where(earlier, 1.0, 0.0), axis=0, keepdims=True)
        alive = target_row >= where_ref[0] + l
        slot = jnp.where(alive, (ids_row * CAP + rank).astype(jnp.int32), -1)
        slot_ref[l : l + 1, :] = slot
        pick = jnp.where(iota((PANELS * CAP, rows), 0) == slot, 1.0, 0.0).astype(BF16)
        sent = jnp.dot(pick, codes_ref[l], preferred_element_type=F32).astype(BF16)
        for h in range(halves):
            half = sent[:, h * LANES : (h + 1) * LANES]
            out_ref[:, h * slots + l * CAP : h * slots + (l + 1) * CAP, :] = half.reshape(PANELS, CAP, LANES)
        named = (iota((PANELS, rows), 0).astype(F32) == ids_row) & alive
        place = jnp.where(iota((rows, LANES), 1) % slots == to_column(rank).astype(jnp.int32) + l * CAP, 1.0, 0.0)
        place = place.astype(BF16)
        token_info += jnp.dot(jnp.where(named, token_row, 0.0).astype(BF16), place, preferred_element_type=F32)
        request_info += jnp.dot(jnp.where(named, request_row, 0.0).astype(BF16), place, preferred_element_type=F32)
    spot = iota((PANELS, LANES), 1) // slots
    token_info = jnp.where(spot == iota((PANELS, LANES), 0) % per, token_info, 0.0)
    request_info = jnp.where(spot == where_ref[1] % per, request_info, 0.0)
    line = iota((PANELS, 8, LANES), 1)
    tile = jnp.where(
        line == 0,
        token_info.reshape(PANELS, 1, LANES),
        jnp.where(line == 1, request_info.reshape(PANELS, 1, LANES), 0.0),
    )
    out_ref[:, halves * slots : halves * slots + 8, :] = tile.astype(BF16)


def build_kernel(codes_ref, weight_ref, out_ref):
    blocks = codes_ref.shape[0]
    layers, panel, width = weight_ref.shape
    slots = layers * CAP
    halves = panel // LANES
    tiles = 2

    def body(n, carry):
        cols = pl.ds(pl.multiple_of(n * tiles * LANES, LANES), tiles * LANES)
        for l in range(layers):
            codes = jnp.concatenate(
                [
                    codes_ref[:, h * slots + l * CAP : h * slots + (l + 1) * CAP, :].reshape(blocks * CAP, LANES)
                    for h in range(halves)
                ],
                axis=1,
            )
            built = jnp.dot(codes, weight_ref[l, :, cols], preferred_element_type=F32).astype(BF16)
            for i in range(tiles):
                at = pl.ds(pl.multiple_of((n * tiles + i) * slots + l * CAP, CAP), CAP)
                out_ref[:, at, :] = built[:, i * LANES : (i + 1) * LANES].reshape(blocks, CAP, LANES)
        return carry

    lax.fori_loop(0, width // (tiles * LANES), body, 0)
    end = width // LANES * slots
    out_ref[:, end : end + 8, :] = codes_ref[:, halves * slots : halves * slots + 8, :]


def reduce_kernel(rows_ref, out_ref, hot_ref):
    groups = rows_ref.shape[0]
    tokens, width = out_ref.shape
    count = hot_ref.shape[0]
    slots = count // groups
    tiles = 2
    end = width // LANES * slots
    token = lane_groups(rows_ref[:, end : end + 8, :].astype(F32)[:, 0:1, :])
    want = (iota((tokens, LANES), 0) + 1).astype(F32)
    hot_t = jnp.concatenate([jnp.where(token[g] == want, 1.0, 0.0) for g in range(count // LANES)], axis=1)
    hot_ref[...] = hot_t.T.astype(BF16)
    hot_t = hot_t.astype(BF16)

    def body(n, carry):
        rows = jnp.concatenate(
            [
                rows_ref[:, pl.ds(pl.multiple_of((n * tiles + i) * slots, slots), slots), :].reshape(count, LANES)
                for i in range(tiles)
            ],
            axis=1,
        )
        cols = pl.ds(pl.multiple_of(n * tiles * LANES, LANES), tiles * LANES)
        out_ref[:, cols] = jnp.dot(hot_t, rows, preferred_element_type=F32).astype(out_ref.dtype)
        return carry

    lax.fori_loop(0, width // (tiles * LANES), body, 0)


def gradient_kernel(parts_ref, resid_ref, out_ref):
    planes, tokens, width = parts_ref.shape
    rebuilt = parts_ref[0].astype(F32)
    for i in range(1, planes):
        rebuilt = rebuilt + parts_ref[i].astype(F32)
    error = resid_ref[...].astype(F32) - rebuilt
    spread = jnp.sum(error * error, axis=-1, keepdims=True) * (1.0 / width)
    gradient = (error * lax.rsqrt(spread + 1e-06)).astype(BF16)
    for i in range(planes):
        out_ref[i] = gradient


def spread_kernel(hot_ref, gradient_ref, out_ref):
    groups = out_ref.shape[0]
    count = hot_ref.shape[0]
    width = gradient_ref.shape[1]
    slots = count // groups
    tiles = 2

    def body(n, carry):
        cols = pl.ds(pl.multiple_of(n * tiles * LANES, LANES), tiles * LANES)
        rows = jnp.dot(hot_ref[...], gradient_ref[:, cols], preferred_element_type=F32).astype(BF16)
        for i in range(tiles):
            at = pl.ds(pl.multiple_of((n * tiles + i) * slots, slots), slots)
            out_ref[:, at, :] = rows[:, i * LANES : (i + 1) * LANES].reshape(groups, slots, LANES)
        return carry

    lax.fori_loop(0, width // (tiles * LANES), body, 0)


def project_kernel(rows_ref, codes_ref, weight_ref, score_ref, total_ref, sum_ref):
    blocks = rows_ref.shape[0]
    layers, panel, width = weight_ref.shape
    slots = layers * CAP
    halves = panel // LANES
    tiles = 2
    sum_ref[...] = jnp.zeros_like(sum_ref)

    def body(n, carry):
        cols = pl.ds(pl.multiple_of(n * tiles * LANES, LANES), tiles * LANES)
        for l in range(layers):
            rows = jnp.concatenate(
                [
                    rows_ref[:, pl.ds(pl.multiple_of((n * tiles + i) * slots + l * CAP, CAP), CAP), :].reshape(
                        blocks * CAP, LANES
                    )
                    for i in range(tiles)
                ],
                axis=1,
            )
            sum_ref[l] += lax.dot_general(
                rows, weight_ref[l, :, cols], (((1,), (1,)), ((), ())), preferred_element_type=F32
            )
        return carry

    lax.fori_loop(0, width // (tiles * LANES), body, 0)
    request = lane_groups(codes_ref[:, halves * slots : halves * slots + 8, :].astype(F32)[:, 1:2, :])
    lane_layer = iota((layers * REQUESTS, LANES), 1) % slots // CAP
    line = iota((layers * REQUESTS, LANES), 0)
    want = (line % REQUESTS + 1).astype(F32)
    here = lane_layer == line // REQUESTS
    member = jnp.concatenate(
        [jnp.where((request[g] == want) & here, 1.0, 0.0) for g in range(blocks * slots // LANES)], axis=1
    ).astype(BF16)
    for h in range(halves):
        values = []
        for l in range(layers):
            at = slice(h * slots + l * CAP, h * slots + (l + 1) * CAP)
            codes = codes_ref[:, at, :].reshape(blocks * CAP, LANES).astype(F32)
            projected = sum_ref[l, :, h * LANES : (h + 1) * LANES].astype(BF16).astype(F32)
            value = codes * projected
            score_ref[:, at, :] = value.astype(BF16).reshape(blocks, CAP, LANES)
            values.append(value.reshape(blocks, CAP, LANES))
        value = jnp.concatenate(values, axis=1).reshape(blocks * slots, LANES)
        upper = value.astype(BF16)
        lower = (value - upper.astype(F32)).astype(BF16)
        summed = jnp.dot(member, upper, preferred_element_type=F32) + jnp.dot(
            member, lower, preferred_element_type=F32
        )
        for l in range(layers):
            total_ref[l, :, h * LANES : (h + 1) * LANES] = summed[l * REQUESTS : (l + 1) * REQUESTS]


def place_kernel(slot_ref, scores_ref, out_ref):
    layers, rows = slot_ref.shape
    slots = layers * CAP
    halves = out_ref.shape[2] // LANES
    for l in range(layers):
        column = to_column(slot_ref[l : l + 1, :])
        pick = jnp.where(iota((rows, PANELS * CAP), 1) == column, 1.0, 0.0).astype(BF16)
        scores = jnp.concatenate(
            [
                scores_ref[:, h * slots + l * CAP : h * slots + (l + 1) * CAP, :].reshape(PANELS * CAP, LANES)
                for h in range(halves)
            ],
            axis=1,
        )
        out_ref[l] = jnp.dot(pick, scores, preferred_element_type=F32).astype(BF16)


def per_device(feature_codes, block_ids, target_layer, request_ids, target_resid, decoder):
    layers, count, kact, panel = feature_codes.shape
    width = target_resid.shape[1]
    rows = count * kact
    blocks = lax.axis_size(TOK)
    planes = lax.axis_size(COLUMN)
    share = count // planes
    slots = layers * CAP
    code_lines = panel // LANES * slots
    row_lines = width // LANES * slots
    zh, zl, y = lax.axis_index("zh"), lax.axis_index("zl"), lax.axis_index("y")
    first_layer = lax.axis_index(LYR) * layers

    sizes = [lax.axis_size(a) for a in EVERY]
    swap = []
    for d in range(sizes[0] * sizes[1] * sizes[2] * sizes[3] * sizes[4]):
        rest, d_y = divmod(d, sizes[4])
        rest, d_zl = divmod(rest, sizes[3])
        d_zh, d_xc = divmod(rest, sizes[1] * sizes[2])
        swap.append((d, ((d_y * sizes[1] * sizes[2] + d_xc) * sizes[3] + d_zl) * sizes[4] + d_zh))
    mine = lax.dynamic_slice_in_dim(target_resid, (y * sizes[3] + zl) * share, share, 0)
    resid = lax.ppermute(mine, EVERY, swap)

    ids = block_ids.transpose(0, 2, 1).reshape(layers, rows)
    codes = feature_codes.transpose(0, 2, 1, 3).reshape(layers, rows, panel)
    where = jnp.stack([first_layer, lax.axis_index(TOK)]).astype(jnp.int32)
    sent, slot = pl.pallas_call(
        pack_kernel,
        out_shape=(
            jax.ShapeDtypeStruct((blocks, code_lines + 8, LANES), BF16),
            jax.ShapeDtypeStruct((layers, rows), jnp.int32),
        ),
        in_specs=[pl.BlockSpec(memory_space=pltpu.SMEM)] + [pl.BlockSpec(memory_space=pltpu.VMEM)] * 4,
        compiler_params=pltpu.CompilerParams(vmem_limit_bytes=12 * 1024 * 1024),
        cost_estimate=pl.CostEstimate(flops=300_000_000, bytes_accessed=1_000_000, transcendentals=0),
    )(where, ids, target_layer.reshape(1, count), request_ids.reshape(1, count), codes)
    codes_in = lax.all_to_all(sent, TOK, 0, 0, tiled=True)

    built = call(
        build_kernel, jax.ShapeDtypeStruct((blocks, row_lines + 8, LANES), BF16), 1_200_000_000, 8_000_000
    )(codes_in, decoder)
    rows_in = lax.all_to_all(built, PLANE, 0, 0, tiled=True)
    partial, hot = call(
        reduce_kernel,
        (jax.ShapeDtypeStruct((count, width), BF16), jax.ShapeDtypeStruct((blocks * slots, count), BF16)),
        600_000_000,
        6_000_000,
    )(rows_in)
    parts = lax.all_to_all(partial.reshape(planes, share, width), COLUMN, 0, 0, tiled=True)
    copies = call(gradient_kernel, jax.ShapeDtypeStruct((planes, share, width), BF16), 1_000_000, 1_200_000)(
        parts, resid
    )
    gradient = lax.all_to_all(copies, COLUMN, 0, 0, tiled=True).reshape(count, width)
    spread = call(spread_kernel, jax.ShapeDtypeStruct((blocks, row_lines, LANES), BF16), 600_000_000, 6_000_000)(
        hot, gradient
    )
    grad_in = lax.all_to_all(spread, PLANE, 0, 0, tiled=True)
    scored, totals = call(
        project_kernel,
        (
            jax.ShapeDtypeStruct((blocks, code_lines, LANES), BF16),
            jax.ShapeDtypeStruct((layers, REQUESTS, panel), F32),
        ),
        1_300_000_000,
        8_000_000,
        [pltpu.VMEM((layers, blocks * CAP, panel), F32)],
    )(grad_in, codes_in, decoder)
    scores_in = lax.all_to_all(scored, TOK, 0, 0, tiled=True)
    placed = call(place_kernel, jax.ShapeDtypeStruct((layers, rows, panel), BF16), 140_000_000, 1_000_000)(
        slot, scores_in
    )
    scores = placed.reshape(layers, kact, count, panel).transpose(0, 2, 1, 3)
    return scores, totals.transpose(1, 0, 2)


def solution(mesh):
    fine = Mesh(mesh.devices.reshape(4, 4, 2, 2, 4), EVERY)
    placed = (
        P(LYR, TOK, None, None),
        P(LYR, TOK, None),
        P(TOK),
        P(TOK),
        P(TOK, None),
        P(LYR, TOK, None),
    )
    return jax.shard_map(
        per_device,
        mesh=fine,
        in_specs=placed,
        out_specs=(P(LYR, TOK, None, None), P(None, LYR, TOK)),
        check_vma=False,
    )
```

time: 267 us -> 250 us (0.936)
  Pallas kernels: 22.1 us -> 14.7 us
  blocking collectives: 190 us -> 183 us
  local copies, waits for them, and re-layouts: 9.68 us -> 6.34 us
    pallas_call x4, Pallas kernels: 19.1 us -> 10.9 us  [the longest x1 4.12 us: per_device(): call(project_kernel, (jax.ShapeDtypeStruct((blocks, code_lines, LANES), B...]
    unnamed x24 -> x12, local copies, waits for them, and re-layouts: 7.68 us -> 4.38 us
    all_to_all x1, blocking collectives: 34.9 us -> 31.6 us  [per_device(): codes_in = lax.all_to_all(sent, TOK, 0, 0, tiled=True)]
    all_to_all x1, blocking collectives: 67.1 us -> 64 us  [per_device(): rows_in = lax.all_to_all(built, PLANE, 0, 0, tiled=True)]
where the time goes in v2:
time: 250 us; the launch traced here: 249 us
  blocking collectives  183 us (73%)
  waiting for transfers between devices  36.4 us (15%)
  Pallas kernels  14.7 us (6%)
  starting transfers between devices  8.19 us (3%)
  local copies, waits for them, and re-layouts  6.34 us (3%)
    all_to_all x1, blocking collectives, per_device(): grad_in = lax.all_to_all(spread, PLANE, 0, 0, tiled=True)  65.2 us
    all_to_all x1, blocking collectives, per_device(): rows_in = lax.all_to_all(built, PLANE, 0, 0, tiled=True)  64 us
    all_to_all x1, blocking collectives, per_device(): codes_in = lax.all_to_all(sent, TOK, 0, 0, tiled=True)  31.6 us
    all_to_all x1, blocking collectives, per_device(): lax.all_to_all(copies, COLUMN, 0, 0, tiled=True).reshape(count, width)  21.8 us
    all_to_all x1, waiting for transfers between devices, per_device(): lax.all_to_all(partial.reshape(planes, share, width), COLUMN, 0, 0, tiled...  18.6 us
    all_to_all x1, waiting for transfers between devices, per_device(): scores_in = lax.all_to_all(scored, TOK, 0, 0, tiled=True)  17.8 us
  transfers between devices with their start and end apart: 3, of which 2 were waited for; matrix products, arithmetic and copies ran while one was open for 0% of the time, Pallas kernels for 0%

profile of v2, /device:TPU:1, one launch (start us, length us, event | category | flops | bytes accessed | tf_op | source)
XLA Modules:
  0.0 249.0 jit_solution(16617680944253099375)
XLA Ops:
  0.6 0.0 copy-start
  0.7 0.7 copy.15
  1.4 1.0 copy.8
  2.4 0.1 pad_add_fusion.where_ref
  2.5 0.0 copy-start.3
  2.5 0.7 copy-done.3
  3.1 0.0 copy-start.4
  3.1 0.7 copy-done.4
  3.8 1.0 shard_map.77
  4.8 31.6 %all_to_all.30.codes_ref = bf16[32,72,128]{2,1,0:T(8,128)(2,1)S(1)} all-to-all(bf16[32,72,128]{2,1,0:T(8,128)(2,1)S(1)} %get-tuple-element.9), channel_id=1, replica_groups=mesh['zh'=4,'x'=4,'c'=2,'zl'=2,'y'=4] {'zh','x','c'}, dimensions={0} | all-to-all | bytes 1179648 | tf_op jit(solution)/shard_map/all_to_all | solution.py:282
  36.5 0.0 copy-start.1
  36.5 1.7 copy-done.1
  38.1 3.0 %shard_map.78 = bf16[32,584,128]{2,1,0:T(8,128)(2,1)S(1)} custom-call(bf16[32,72,128]{2,1,0:T(8,128)(2,1)S(1)} %all_to_all.30.codes_ref, bf16[2,256,2304]{2,1,0:T(8,128)(2,1)S(1)} %copy-done.1), custom_call_target="tpu_custom_call" | custom-call | flops 1200000000 | bytes 8000000 | tf_op jit(solution)/shard_map/pallas_call | solution.py:284
  41.2 64.0 %all_to_all.31.rows_ref = bf16[32,584,128]{2,1,0:T(8,128)(2,1)S(1)} all-to-all(bf16[32,584,128]{2,1,0:T(8,128)(2,1)S(1)} %shard_map.78), channel_id=1, replica_groups=mesh['zh'=4,'x'=4,'c'=2,'zl'=2,'y'=4] {'y','x','c'}, dimensions={0} | all-to-all | bytes 9568256 | tf_op jit(solution)/shard_map/all_to_all | solution.py:287
  105.2 3.1 %shard_map.79 = (bf16[128,2304]{1,0:T(8,128)(2,1)}, bf16[1024,128]{1,0:T(8,128)(2,1)S(1)}) custom-call(bf16[32,584,128]{2,1,0:T(8,128)(2,1)S(1)} %all_to_all.31.rows_ref), custom_call_target="tpu_custom_call" | custom-call | flops 600000000 | bytes 6000000 | tf_op jit(solution)/shard_map/pallas_call | solution.py:288
  108.3 3.5 %all-to-all-start.2 = ((bf16[8,16,2304]{2,1,0:T(8,128)(2,1)}), bf16[8,16,2304]{2,1,0:T(8,128)(2,1)S(1)}, u32[]{:S(2)}, u32[]{:S(2)}) async-start(bf16[8,16,2304]{2,1,0:T(8,128)(2,1)} %bitcast.7), calls=%async_computation.2 | async-start | bytes 1179648 | tf_op jit(solution)/shard_map/all_to_all | solution.py:294
  111.9 0.0 copy-done
  111.9 0.7 collective-permute-start
  112.6 0.0 collective-permute-done.resid_ref
  112.6 18.6 %all-to-all-done.2.parts_ref = bf16[8,16,2304]{2,1,0:T(8,128)(2,1)S(1)} async-done(((bf16[8,16,2304]{2,1,0:T(8,128)(2,1)}), bf16[8,16,2304]{2,1,0:T(8,128)(2,1)S(1)}, u32[]{:S(2)}, u32[]{:S(2)}) %all-to-all-start.2) | async-done | bytes 589856 | tf_op jit(solution)/shard_map/all_to_all | solution.py:294
  131.2 0.2 shard_map.80
  131.4 21.8 %all_to_all.32 = bf16[8,16,2304]{2,1,0:T(8,128)(2,1)S(1)} all-to-all(bf16[8,16,2304]{2,1,0:T(8,128)(2,1)S(1)} %shard_map.80), channel_id=1, replica_groups=mesh['zh'=4,'x'=4,'c'=2,'zl'=2,'y'=4] {'zh','zl'}, dimensions={0} | all-to-all | bytes 1179648 | tf_op jit(solution)/shard_map/all_to_all | solution.py:298
  153.1 2.7 %shard_map.81 = bf16[32,576,128]{2,1,0:T(8,128)(2,1)S(1)} custom-call(bf16[1024,128]{1,0:T(8,128)(2,1)S(1)} %get-tuple-element.10.hot_ref, bf16[128,2304]{1,0:T(8,128)(2,1)S(1)} %bitcast.18), custom_call_target="tpu_custom_call" | custom-call | flops 600000000 | bytes 6000000 | tf_op jit(solution)/shard_map/pallas_call | solution.py:299
  155.8 0.0 copy-start.2
  155.9 65.2 %all_to_all.33.rows_ref = bf16[32,576,128]{2,1,0:T(8,128)(2,1)S(1)} all-to-all(bf16[32,576,128]{2,1,0:T(8,128)(2,1)S(1)} %shard_map.81), channel_id=1, replica_groups=mesh['zh'=4,'x'=4,'c'=2,'zl'=2,'y'=4] {'y','x','c'}, dimensions={0} | all-to-all | bytes 9437184 | tf_op jit(solution)/shard_map/all_to_all | solution.py:302
  221.0 0.0 copy-done.2
  221.0 4.1 %shard_map.82 = (bf16[32,64,128]{2,1,0:T(8,128)(2,1)}, f32[2,16,256]{2,1,0:T(8,128)S(1)}) custom-call(bf16[32,576,128]{2,1,0:T(8,128)(2,1)S(1)} %all_to_all.33.rows_ref, bf16[32,72,128]{2,1,0:T(8,128)(2,1)S(1)} %all_to_all.30.codes_ref, bf16[2,256,2304]{2,1,0:T(8,128)(2,1)S(1)} %copy-done.2), custom_call_target="tpu_custom_call" | custom-call | flops 1300000000 | bytes 8000000 | tf_op jit(solution)/shard_map/pallas_call | solution.py:303
  225.2 4.0 %all-to-all-start.5 = ((bf16[32,64,128]{2,1,0:T(8,128)(2,1)}), bf16[32,64,128]{2,1,0:T(8,128)(2,1)S(1)}, u32[]{:S(2)}, u32[]{:S(2)}) async-start(bf16[32,64,128]{2,1,0:T(8,128)(2,1)} %get-tuple-element.12), calls=%async_computation.5 | async-start | bytes 1048576 | tf_op jit(solution)/shard_map/all_to_all | solution.py:313
  229.1 0.6 copy.10
  229.8 17.8 %all-to-all-done.5.scores_ref = bf16[32,64,128]{2,1,0:T(8,128)(2,1)S(1)} async-done(((bf16[32,64,128]{2,1,0:T(8,128)(2,1)}), bf16[32,64,128]{2,1,0:T(8,128)(2,1)S(1)}, u32[]{:S(2)}, u32[]{:S(2)}) %all-to-all-start.5) | async-done | bytes 524320 | tf_op jit(solution)/shard_map/all_to_all | solution.py:313
  247.6 0.4 shard_map.83
  248.0 1.0 copy.14
  (1 shorter events, 0.0 us)
Async XLA Ops:
  0.6 111.2 %copy-start = (bf16[128,2304]{1,0:T(8,128)(2,1)S(1)}, bf16[128,2304]{1,0:T(8,128)(2,1)}, u32[]{:S(2)}) copy-start(bf16[128,2304]{1,0:T(8,128)(2,1)} %param.10) | copy-start | bytes 1769476
  2.5 0.7 copy-start.3
  3.1 0.7 copy-start.4
  36.5 1.7 copy-start.1
  108.3 22.8 %all-to-all-start.2 = ((bf16[8,16,2304]{2,1,0:T(8,128)(2,1)}), bf16[8,16,2304]{2,1,0:T(8,128)(2,1)S(1)}, u32[]{:S(2)}, u32[]{:S(2)}) async-start(bf16[8,16,2304]{2,1,0:T(8,128)(2,1)} %bitcast.7), calls=%async_computation.2 | async-start | bytes 1179648 | tf_op jit(solution)/shard_map/all_to_all | solution.py:294
  111.9 0.7 collective-permute-start
  155.8 65.2 %copy-start.2 = (bf16[2,256,2304]{2,1,0:T(8,128)(2,1)S(1)}, bf16[2,256,2304]{2,1,0:T(8,128)(2,1)}, u32[]{:S(2)}) copy-start(bf16[2,256,2304]{2,1,0:T(8,128)(2,1)} %weight_ref.3) | copy-start | bytes 7077892
  225.2 22.5 %all-to-all-start.5 = ((bf16[32,64,128]{2,1,0:T(8,128)(2,1)}), bf16[32,64,128]{2,1,0:T(8,128)(2,1)S(1)}, u32[]{:S(2)}, u32[]{:S(2)}) async-start(bf16[32,64,128]{2,1,0:T(8,128)(2,1)} %get-tuple-element.12), calls=%async_computation.5 | async-start | bytes 1048576 | tf_op jit(solution)/shard_map/all_to_all | solution.py:313

commit v3 on v2

v3 whole, which is shorter than its diff:
```python
import jax
import jax.numpy as jnp
from jax import lax
from jax.experimental import pallas as pl
from jax.experimental.pallas import tpu as pltpu
from jax.sharding import Mesh, PartitionSpec as P

PANELS = 32
REQUESTS = 16
CAP = 16
LANES = 128
TOK = ("zh", "x", "c")
SPREAD = ("x", "zh", "c")
LYR = ("zl", "y")
PLANE = ("x", "y", "c")
COLUMN = ("zl", "zh")
EVERY = ("zh", "x", "c", "zl", "y")
BF16 = jnp.bfloat16
F32 = jnp.float32


def call(kernel, out_shape, flops, moved, scratch=(), limit=10):
    return pl.pallas_call(
        kernel,
        out_shape=out_shape,
        scratch_shapes=list(scratch),
        compiler_params=pltpu.CompilerParams(vmem_limit_bytes=limit * 1024 * 1024),
        cost_estimate=pl.CostEstimate(flops=flops, bytes_accessed=moved, transcendentals=0),
    )


def iota(shape, axis):
    return lax.broadcasted_iota(jnp.int32, shape, axis)


def to_column(row):
    n = row.shape[1]
    diag = iota((n, n), 0) == iota((n, n), 1)
    return jnp.sum(jnp.where(diag, jnp.broadcast_to(row, (n, n)), jnp.zeros((n, n), row.dtype)), axis=1, keepdims=True)


def lane_groups(info):
    groups = info.shape[0]
    return jnp.sum(info.reshape(groups // 4, 4, 1, LANES), axis=1)


def pack_kernel(small_ref, codes_ref, out_ref, slot_ref):
    layers, rows, panel = codes_ref.shape
    tokens = small_ref.shape[1]
    kact = rows // tokens
    first_layer = lax.axis_index(LYR) * layers
    slots = layers * CAP
    per = LANES // slots
    halves = panel // LANES
    target = small_ref[layers * kact : layers * kact + 1, :]
    request = small_ref[layers * kact + 1 : layers * kact + 2, :].astype(F32) + 1.0
    target_row = jnp.concatenate([target] * kact, axis=1)
    request_row = jnp.concatenate([request] * kact, axis=1)
    token_row = (iota((1, rows), 1) % tokens + 1).astype(F32)
    token_info = jnp.zeros((PANELS, LANES), F32)
    request_info = jnp.zeros((PANELS, LANES), F32)
    for l in range(layers):
        panel_id = jnp.concatenate([small_ref[l * kact + k : l * kact + k + 1, :] for k in range(kact)], axis=1)
        zh, x, c = panel_id // 8, panel_id // 2 % 4, panel_id % 2
        ids_row = (x * 8 + zh * 2 + c).astype(F32)
        ids_col = to_column(ids_row)
        earlier = (ids_col == ids_row) & (iota((rows, rows), 0) < iota((rows, rows), 1))
        rank = jnp.sum(jnp.where(earlier, 1.0, 0.0), axis=0, keepdims=True)
        alive = target_row >= first_layer + l
        slot = jnp.where(alive, (ids_row * CAP + rank).astype(jnp.int32), -1)
        slot_ref[l : l + 1, :] = slot
        pick = jnp.where(iota((PANELS * CAP, rows), 0) == slot, 1.0, 0.0).astype(BF16)
        sent = jnp.dot(pick, codes_ref[l], preferred_element_type=F32).astype(BF16)
        for h in range(halves):
            half = sent[:, h * LANES : (h + 1) * LANES]
            out_ref[:, h * slots + l * CAP : h * slots + (l + 1) * CAP, :] = half.reshape(PANELS, CAP, LANES)
        named = (iota((PANELS, rows), 0).astype(F32) == ids_row) & alive
        place = jnp.where(iota((rows, LANES), 1) % slots == to_column(rank).astype(jnp.int32) + l * CAP, 1.0, 0.0)
        place = place.astype(BF16)
        token_info += jnp.dot(jnp.where(named, token_row, 0.0).astype(BF16), place, preferred_element_type=F32)
        request_info += jnp.dot(jnp.where(named, request_row, 0.0).astype(BF16), place, preferred_element_type=F32)
    spot = iota((PANELS, LANES), 1) // slots
    sender = lax.axis_index("y") % 2 * 2 + iota((PANELS, LANES), 0) % 2
    token_info = jnp.where(spot == sender, token_info, 0.0)
    request_info = jnp.where(spot == lax.axis_index(SPREAD) % per, request_info, 0.0)
    line = iota((PANELS, 8, LANES), 1)
    tile = jnp.where(
        line == 0,
        token_info.reshape(PANELS, 1, LANES),
        jnp.where(line == 1, request_info.reshape(PANELS, 1, LANES), 0.0),
    )
    out_ref[:, halves * slots : halves * slots + 8, :] = tile.astype(BF16)


def build_kernel(codes_ref, weight_ref, out_ref):
    blocks = codes_ref.shape[0]
    layers, panel, width = weight_ref.shape
    slots = layers * CAP
    halves = panel // LANES
    step = 2 * LANES
    for l in range(layers):
        codes = jnp.concatenate(
            [
                codes_ref[:, h * slots + l * CAP : h * slots + (l + 1) * CAP, :].reshape(blocks * CAP, LANES)
                for h in range(halves)
            ],
            axis=1,
        )
        for n in range(0, width, step):
            built = jnp.dot(codes, weight_ref[l, :, n : n + step], preferred_element_type=F32).astype(BF16)
            for i in range(0, step, LANES):
                at = (n + i) // LANES * slots + l * CAP
                out_ref[:, at : at + CAP, :] = built[:, i : i + LANES].reshape(blocks, CAP, LANES)
    end = width // LANES * slots
    out_ref[:, end : end + 8, :] = codes_ref[:, halves * slots : halves * slots + 8, :]


def reduce_kernel(rows_ref, resid_ref, out_ref, hot_ref):
    groups = rows_ref.shape[0]
    tokens, width = out_ref.shape
    count = hot_ref.shape[0]
    slots = count // groups
    step = 2 * LANES
    end = width // LANES * slots
    token = lane_groups(rows_ref[:, end : end + 8, :].astype(F32)[:, 0:1, :])
    want = (iota((tokens, LANES), 0) + 1).astype(F32)
    hot_t = jnp.concatenate([jnp.where(token[g] == want, 1.0, 0.0) for g in range(count // LANES)], axis=1)
    hot_ref[...] = hot_t.T.astype(BF16)
    hot_t = hot_t.astype(BF16)
    home = (lax.axis_index("zh") == lax.axis_index("y")) & (lax.axis_index("zl") == 0)
    share = jnp.where(home, 1.0, 0.0)
    for n in range(0, width, step):
        rows = jnp.concatenate(
            [
                rows_ref[:, (n + i) // LANES * slots : (n + i) // LANES * slots + slots, :].reshape(count, LANES)
                for i in range(0, step, LANES)
            ],
            axis=1,
        )
        summed = jnp.dot(hot_t, rows, preferred_element_type=F32)
        out_ref[:, n : n + step] = (summed - share * resid_ref[:, n : n + step].astype(F32)).astype(out_ref.dtype)


def gradient_kernel(parts_ref, out_ref):
    planes, tokens, width = parts_ref.shape
    missing = parts_ref[0].astype(F32)
    for i in range(1, planes):
        missing = missing + parts_ref[i].astype(F32)
    error = -missing
    spread = jnp.sum(error * error, axis=-1, keepdims=True) * (1.0 / width)
    gradient = (error * lax.rsqrt(spread + 1e-06)).astype(BF16)
    for i in range(planes):
        out_ref[i] = gradient


def spread_kernel(hot_ref, gradient_ref, out_ref):
    groups = out_ref.shape[0]
    count = hot_ref.shape[0]
    width = gradient_ref.shape[1]
    slots = count // groups
    step = 2 * LANES
    for n in range(0, width, step):
        rows = jnp.dot(hot_ref[...], gradient_ref[:, n : n + step], preferred_element_type=F32).astype(BF16)
        for i in range(0, step, LANES):
            at = (n + i) // LANES * slots
            out_ref[:, at : at + slots, :] = rows[:, i : i + LANES].reshape(groups, slots, LANES)


def project_kernel(rows_ref, codes_ref, weight_ref, score_ref, total_ref):
    blocks = rows_ref.shape[0]
    layers, panel, width = weight_ref.shape
    slots = layers * CAP
    halves = panel // LANES
    projections = []
    for l in range(layers):
        rows = jnp.concatenate(
            [
                rows_ref[:, n * slots + l * CAP : n * slots + (l + 1) * CAP, :].reshape(blocks * CAP, LANES)
                for n in range(width // LANES)
            ],
            axis=1,
        )
        projections.append(
            lax.dot_general(rows, weight_ref[l], (((1,), (1,)), ((), ())), preferred_element_type=F32).astype(BF16)
        )
    request = lane_groups(codes_ref[:, halves * slots : halves * slots + 8, :].astype(F32)[:, 1:2, :])
    lane_layer = iota((layers * REQUESTS, LANES), 1) % slots // CAP
    line = iota((layers * REQUESTS, LANES), 0)
    want = (line % REQUESTS + 1).astype(F32)
    here = lane_layer == line // REQUESTS
    member = jnp.concatenate(
        [jnp.where((request[g] == want) & here, 1.0, 0.0) for g in range(blocks * slots // LANES)], axis=1
    ).astype(BF16)
    for h in range(halves):
        values = []
        for l in range(layers):
            at = slice(h * slots + l * CAP, h * slots + (l + 1) * CAP)
            codes = codes_ref[:, at, :].reshape(blocks * CAP, LANES).astype(F32)
            projected = projections[l][:, h * LANES : (h + 1) * LANES].astype(F32)
            value = codes * projected
            score_ref[:, at, :] = value.astype(BF16).reshape(blocks, CAP, LANES)
            values.append(value.reshape(blocks, CAP, LANES))
        value = jnp.concatenate(values, axis=1).reshape(blocks * slots, LANES)
        upper = value.astype(BF16)
        lower = (value - upper.astype(F32)).astype(BF16)
        summed = jnp.dot(member, upper, preferred_element_type=F32) + jnp.dot(
            member, lower, preferred_element_type=F32
        )
        for l in range(layers):
            total_ref[:, l, h * LANES : (h + 1) * LANES] = summed[l * REQUESTS : (l + 1) * REQUESTS]


def place_kernel(slot_ref, scores_ref, out_ref):
    layers, rows = slot_ref.shape
    slots = layers * CAP
    halves = out_ref.shape[2] // LANES
    for l in range(layers):
        column = to_column(slot_ref[l : l + 1, :])
        pick = jnp.where(iota((rows, PANELS * CAP), 1) == column, 1.0, 0.0).astype(BF16)
        scores = jnp.concatenate(
            [
                scores_ref[:, h * slots + l * CAP : h * slots + (l + 1) * CAP, :].reshape(PANELS * CAP, LANES)
                for h in range(halves)
            ],
            axis=1,
        )
        out_ref[l] = jnp.dot(pick, scores, preferred_element_type=F32).astype(BF16)


def per_device(feature_codes, block_ids, target_layer, request_ids, target_resid, decoder):
    layers, count, kact, panel = feature_codes.shape
    width = target_resid.shape[1]
    rows = count * kact
    blocks = lax.axis_size(TOK)
    planes = lax.axis_size(COLUMN)
    share = count // planes
    slots = layers * CAP
    code_lines = panel // LANES * slots
    row_lines = width // LANES * slots
    small = jnp.concatenate(
        [
            block_ids.transpose(0, 2, 1).reshape(layers * kact, count),
            target_layer.reshape(1, count),
            request_ids.reshape(1, count),
        ],
        axis=0,
    )
    codes = feature_codes.transpose(0, 2, 1, 3).reshape(layers, rows, panel)
    sent, slot = call(
        pack_kernel,
        (
            jax.ShapeDtypeStruct((blocks, code_lines + 8, LANES), BF16),
            jax.ShapeDtypeStruct((layers, rows), jnp.int32),
        ),
        300_000_000,
        4_000_000,
    )(small, codes)
    codes_in = lax.all_to_all(sent, SPREAD, 0, 0, tiled=True)

    built = call(
        build_kernel, jax.ShapeDtypeStruct((blocks, row_lines + 8, LANES), BF16), 1_200_000_000, 8_000_000
    )(codes_in, decoder)
    rows_in = lax.all_to_all(built, PLANE, 0, 0, tiled=True)
    partial, hot = call(
        reduce_kernel,
        (jax.ShapeDtypeStruct((count, width), BF16), jax.ShapeDtypeStruct((blocks * slots, count), BF16)),
        600_000_000,
        6_000_000,
    )(rows_in, target_resid)
    parts = lax.all_to_all(partial.reshape(planes, share, width), COLUMN, 0, 0, tiled=True)
    copies = call(gradient_kernel, jax.ShapeDtypeStruct((planes, share, width), BF16), 1_000_000, 1_200_000)(
        parts
    )
    gradient = lax.all_to_all(copies, COLUMN, 0, 0, tiled=True).reshape(count, width)
    spread = call(spread_kernel, jax.ShapeDtypeStruct((blocks, row_lines, LANES), BF16), 600_000_000, 6_000_000)(
        hot, gradient
    )
    grad_in = lax.all_to_all(spread, PLANE, 0, 0, tiled=True)
    scored, totals = call(
        project_kernel,
        (
            jax.ShapeDtypeStruct((blocks, code_lines, LANES), BF16),
            jax.ShapeDtypeStruct((REQUESTS, layers, panel), F32),
        ),
        1_300_000_000,
        8_000_000,
    )(grad_in, codes_in, decoder)
    scores_in = lax.all_to_all(scored, SPREAD, 0, 0, tiled=True)
    placed = call(place_kernel, jax.ShapeDtypeStruct((layers, rows, panel), BF16), 140_000_000, 1_000_000)(
        slot, scores_in
    )
    scores = placed.reshape(layers, kact, count, panel).transpose(0, 2, 1, 3)
    return scores, totals


def solution(mesh):
    fine = Mesh(mesh.devices.reshape(4, 4, 2, 2, 4), EVERY)
    placed = (
        P(LYR, TOK, None, None),
        P(LYR, TOK, None),
        P(TOK),
        P(TOK),
        P(TOK, None),
        P(LYR, TOK, None),
    )
    return jax.shard_map(
        per_device,
        mesh=fine,
        in_specs=placed,
        out_specs=(P(LYR, TOK, None, None), P(None, LYR, TOK)),
        check_vma=False,
    )
```

time: 250 us -> 231 us (0.924)
  waiting for transfers between devices: 36.4 us -> 0 us
  blocking collectives: 183 us -> 218 us
  starting transfers between devices: 8.19 us -> 0 us
  Pallas kernels: 14.7 us -> 7.06 us
  local copies, waits for them, and re-layouts: 6.34 us -> 3.63 us
    all_to_all x1 -> x3, blocking collectives: 31.6 us -> 71 us  [the longest x1 31.4 us: per_device(): codes_in = lax.all_to_all(sent, SPREAD, 0, 0, tiled=True)]
    all_to_all x2 -> x0, waiting for transfers between devices: 36.4 us -> none  [the longest x1 18.6 us: per_device(): lax.all_to_all(partial.reshape(planes, share, width), COLUMN, 0, 0, tiled...]
    all_to_all x2 -> x0, starting transfers between devices: 7.52 us -> none  [the longest x1 3.99 us: per_device(): scores_in = lax.all_to_all(scored, TOK, 0, 0, tiled=True)]
    unnamed x12 -> x6, local copies, waits for them, and re-layouts: 4.38 us -> 1.68 us
  transfers between devices with their start and end apart: 3 -> 0, of which waited for: 2 -> 0; matrix products, arithmetic and copies ran while one was open for 0% -> 0% of each run, Pallas kernels for 0% -> 0%
where the time goes in v3:
time: 231 us; the launch traced here: 230 us
  blocking collectives  218 us (94%)
  Pallas kernels  7.06 us (3%)
  local copies, waits for them, and re-layouts  3.63 us (2%)
    all_to_all x1, blocking collectives, per_device(): rows_in = lax.all_to_all(built, PLANE, 0, 0, tiled=True)  64.2 us
    all_to_all x1, blocking collectives, per_device(): grad_in = lax.all_to_all(spread, PLANE, 0, 0, tiled=True)  63.2 us
    all_to_all x1, blocking collectives, per_device(): codes_in = lax.all_to_all(sent, SPREAD, 0, 0, tiled=True)  31.4 us
    all_to_all x1, blocking collectives, per_device(): scores_in = lax.all_to_all(scored, SPREAD, 0, 0, tiled=True)  20.3 us
    all_to_all x1, blocking collectives, per_device(): lax.all_to_all(copies, COLUMN, 0, 0, tiled=True).reshape(count, width)  19.9 us
    all_to_all x1, blocking collectives, per_device(): lax.all_to_all(partial.reshape(planes, share, width), COLUMN, 0, 0, tiled...  19.3 us

profile of v3, /device:TPU:1, one launch (start us, length us, event | category | flops | bytes accessed | tf_op | source)
XLA Modules:
  0.0 230.4 jit_solution(1343231975091495905)
XLA Ops:
  0.6 1.0 copy.8
  1.6 0.7 pad_add_fusion.small_ref
  2.3 0.5 shard_map.77
  2.9 31.4 %all_to_all.30.codes_ref = bf16[32,72,128]{2,1,0:T(8,128)(2,1)S(1)} all-to-all(bf16[32,72,128]{2,1,0:T(8,128)(2,1)S(1)} %get-tuple-element.9), channel_id=1, replica_groups=mesh['zh'=4,'x'=4,'c'=2,'zl'=2,'y'=4] {'x','zh','c'}, dimensions={0} | all-to-all | bytes 1179648 | tf_op jit(solution)/shard_map/all_to_all | solution.py:258
  34.2 0.0 copy-start
  34.2 1.7 copy-done
  35.9 1.4 shard_map.78
  37.3 0.0 copy-start.2
  37.3 64.2 %all_to_all.31.rows_ref = bf16[32,584,128]{2,1,0:T(8,128)(2,1)S(1)} all-to-all(bf16[32,584,128]{2,1,0:T(8,128)(2,1)S(1)} %shard_map.78), channel_id=1, replica_groups=mesh['zh'=4,'x'=4,'c'=2,'zl'=2,'y'=4] {'x','y','c'}, dimensions={0} | all-to-all | bytes 9568256 | tf_op jit(solution)/shard_map/all_to_all | solution.py:263
  101.5 0.0 copy-done.2
  101.5 0.8 shard_map.79
  102.3 19.3 %all_to_all.32.parts_ref = bf16[8,16,2304]{2,1,0:T(8,128)(2,1)S(1)} all-to-all(bf16[8,16,2304]{2,1,0:T(8,128)(2,1)S(1)} %bitcast.15), channel_id=1, replica_groups=mesh['zh'=4,'x'=4,'c'=2,'zl'=2,'y'=4] {'zl','zh'}, dimensions={0} | all-to-all | bytes 1179648 | tf_op jit(solution)/shard_map/all_to_all | solution.py:270
  121.7 0.2 shard_map.80
  121.9 19.9 %all_to_all.33 = bf16[8,16,2304]{2,1,0:T(8,128)(2,1)S(1)} all-to-all(bf16[8,16,2304]{2,1,0:T(8,128)(2,1)S(1)} %shard_map.80), channel_id=1, replica_groups=mesh['zh'=4,'x'=4,'c'=2,'zl'=2,'y'=4] {'zl','zh'}, dimensions={0} | all-to-all | bytes 1179648 | tf_op jit(solution)/shard_map/all_to_all | solution.py:274
  141.7 1.4 shard_map.81
  143.1 0.0 copy-start.1
  143.1 63.2 %all_to_all.34.rows_ref = bf16[32,576,128]{2,1,0:T(8,128)(2,1)S(1)} all-to-all(bf16[32,576,128]{2,1,0:T(8,128)(2,1)S(1)} %shard_map.81), channel_id=1, replica_groups=mesh['zh'=4,'x'=4,'c'=2,'zl'=2,'y'=4] {'x','y','c'}, dimensions={0} | all-to-all | bytes 9437184 | tf_op jit(solution)/shard_map/all_to_all | solution.py:278
  206.3 0.0 copy-done.1
  206.3 2.4 %shard_map.82 = (bf16[32,64,128]{2,1,0:T(8,128)(2,1)S(1)}, f32[16,2,256]{2,1,0:T(2,128)}) custom-call(bf16[32,576,128]{2,1,0:T(8,128)(2,1)S(1)} %all_to_all.34.rows_ref, bf16[32,72,128]{2,1,0:T(8,128)(2,1)S(1)} %all_to_all.30.codes_ref, bf16[2,256,2304]{2,1,0:T(8,128)(2,1)S(1)} %copy-done.1), custom_call_target="tpu_custom_call" | custom-call | flops 1300000000 | bytes 8000000 | tf_op jit(solution)/shard_map/pallas_call | solution.py:279
  208.7 20.3 %all_to_all.35.scores_ref = bf16[32,64,128]{2,1,0:T(8,128)(2,1)S(1)} all-to-all(bf16[32,64,128]{2,1,0:T(8,128)(2,1)S(1)} %get-tuple-element.12), channel_id=1, replica_groups=mesh['zh'=4,'x'=4,'c'=2,'zl'=2,'y'=4] {'x','zh','c'}, dimensions={0} | all-to-all | bytes 1048576 | tf_op jit(solution)/shard_map/all_to_all | solution.py:288
  229.0 0.4 shard_map.83
  229.4 1.0 copy.11
Async XLA Ops:
  34.2 1.7 copy-start
  37.3 64.2 %copy-start.2 = (bf16[128,2304]{1,0:T(8,128)(2,1)S(1)}, bf16[128,2304]{1,0:T(8,128)(2,1)}, u32[]{:S(2)}) copy-start(bf16[128,2304]{1,0:T(8,128)(2,1)} %resid_ref.1) | copy-start | bytes 1769476
  143.1 63.2 %copy-start.1 = (bf16[2,256,2304]{2,1,0:T(8,128)(2,1)S(1)}, bf16[2,256,2304]{2,1,0:T(8,128)(2,1)}, u32[]{:S(2)}) copy-start(bf16[2,256,2304]{2,1,0:T(8,128)(2,1)} %weight_ref.3) | copy-start | bytes 7077892

commit v4 on v3

--- a/solution.py
+++ b/solution.py
@@ -44,23 +44,45 @@
     return jnp.sum(info.reshape(groups // 4, 4, 1, LANES), axis=1)
 
 
-def pack_kernel(small_ref, codes_ref, out_ref, slot_ref):
-    layers, rows, panel = codes_ref.shape
-    tokens = small_ref.shape[1]
-    kact = rows // tokens
+def pack_kernel(
+    ids_hbm, target_hbm, request_hbm, codes_hbm, weight_hbm,
+    out_ref, slot_ref, weight_out,
+    ids_ref, target_ref, request_ref, codes_ref, sems,
+):
+    pairs = (
+        (ids_hbm, ids_ref), (target_hbm, target_ref), (request_hbm, request_ref), (codes_hbm, codes_ref),
+        (weight_hbm, weight_out),
+    )
+    loads = [pltpu.make_async_copy(source, held, sems.at[i]) for i, (source, held) in enumerate(pairs)]
+    for load in loads:
+        load.start()
+    for load in loads[:-2]:
+        load.wait()
+    layers, tokens, kact, panel = codes_ref.shape
+    rows = kact * tokens
     first_layer = lax.axis_index(LYR) * layers
     slots = layers * CAP
     per = LANES // slots
     halves = panel // LANES
-    target = small_ref[layers * kact : layers * kact + 1, :]
-    request = small_ref[layers * kact + 1 : layers * kact + 2, :].astype(F32) + 1.0
-    target_row = jnp.concatenate([target] * kact, axis=1)
-    request_row = jnp.concatenate([request] * kact, axis=1)
-    token_row = (iota((1, rows), 1) % tokens + 1).astype(F32)
+    small = jnp.concatenate([ids_ref[l] for l in range(layers)] + [target_ref[...], request_ref[...]], axis=0)
+    small = small.astype(F32).astype(BF16)
+    spaced = [
+        jnp.dot(
+            small,
+            jnp.where(iota((tokens, rows), 1) == iota((tokens, rows), 0) * kact + k, 1.0, 0.0).astype(BF16),
+            preferred_element_type=F32,
+        )
+        for k in range(kact)
+    ]
+    at = layers * kact
+    target_row = sum(part[at : at + 1] for part in spaced).astype(jnp.int32)
+    request_row = sum(part[at + 1 : at + 2] for part in spaced) + 1.0
+    token_row = (iota((1, rows), 1) // kact + 1).astype(F32)
+    loads[-2].wait()
     token_info = jnp.zeros((PANELS, LANES), F32)
     request_info = jnp.zeros((PANELS, LANES), F32)
     for l in range(layers):
-        panel_id = jnp.concatenate([small_ref[l * kact + k : l * kact + k + 1, :] for k in range(kact)], axis=1)
+        panel_id = sum(spaced[k][l * kact + k : l * kact + k + 1] for k in range(kact)).astype(jnp.int32)
         zh, x, c = panel_id // 8, panel_id // 2 % 4, panel_id % 2
         ids_row = (x * 8 + zh * 2 + c).astype(F32)
         ids_col = to_column(ids_row)
@@ -70,7 +92,7 @@
         slot = jnp.where(alive, (ids_row * CAP + rank).astype(jnp.int32), -1)
         slot_ref[l : l + 1, :] = slot
         pick = jnp.where(iota((PANELS * CAP, rows), 0) == slot, 1.0, 0.0).astype(BF16)
-        sent = jnp.dot(pick, codes_ref[l], preferred_element_type=F32).astype(BF16)
+        sent = jnp.dot(pick, codes_ref[l].reshape(rows, panel), preferred_element_type=F32).astype(BF16)
         for h in range(halves):
             half = sent[:, h * LANES : (h + 1) * LANES]
             out_ref[:, h * slots + l * CAP : h * slots + (l + 1) * CAP, :] = half.reshape(PANELS, CAP, LANES)
@@ -90,6 +112,7 @@
         jnp.where(line == 1, request_info.reshape(PANELS, 1, LANES), 0.0),
     )
     out_ref[:, halves * slots : halves * slots + 8, :] = tile.astype(BF16)
+    loads[-1].wait()
 
 
 def build_kernel(codes_ref, weight_ref, out_ref):
@@ -213,7 +236,7 @@
 def place_kernel(slot_ref, scores_ref, out_ref):
     layers, rows = slot_ref.shape
     slots = layers * CAP
-    halves = out_ref.shape[2] // LANES
+    halves = out_ref.shape[3] // LANES
     for l in range(layers):
         column = to_column(slot_ref[l : l + 1, :])
         pick = jnp.where(iota((rows, PANELS * CAP), 1) == column, 1.0, 0.0).astype(BF16)
@@ -224,7 +247,8 @@
             ],
             axis=1,
         )
-        out_ref[l] = jnp.dot(pick, scores, preferred_element_type=F32).astype(BF16)
+        placed = jnp.dot(pick, scores, preferred_element_type=F32).astype(BF16)
+        out_ref[l] = placed.reshape(out_ref.shape[1:])
 
 
 def per_device(feature_codes, block_ids, target_layer, request_ids, target_resid, decoder):
@@ -237,29 +261,33 @@
     slots = layers * CAP
     code_lines = panel // LANES * slots
     row_lines = width // LANES * slots
-    small = jnp.concatenate(
-        [
-            block_ids.transpose(0, 2, 1).reshape(layers * kact, count),
-            target_layer.reshape(1, count),
-            request_ids.reshape(1, count),
-        ],
-        axis=0,
-    )
-    codes = feature_codes.transpose(0, 2, 1, 3).reshape(layers, rows, panel)
-    sent, slot = call(
+    offchip = pl.BlockSpec(memory_space=pltpu.HBM)
+    onchip = pl.BlockSpec(memory_space=pltpu.VMEM)
+    held = (
+        block_ids.transpose(0, 2, 1),
+        target_layer.reshape(1, count),
+        request_ids.reshape(1, count),
+        feature_codes,
+        decoder,
+    )
+    sent, slot, weights = pl.pallas_call(
         pack_kernel,
-        (
+        out_shape=(
             jax.ShapeDtypeStruct((blocks, code_lines + 8, LANES), BF16),
             jax.ShapeDtypeStruct((layers, rows), jnp.int32),
+            jax.ShapeDtypeStruct(decoder.shape, decoder.dtype),
         ),
-        300_000_000,
-        4_000_000,
-    )(small, codes)
+        in_specs=[offchip] * len(held),
+        out_specs=(onchip, onchip, pl.BlockSpec(memory_space=pl.ANY)),
+        scratch_shapes=[pltpu.VMEM(a.shape, a.dtype) for a in held[:-1]] + [pltpu.SemaphoreType.DMA((len(held),))],
+        compiler_params=pltpu.CompilerParams(vmem_limit_bytes=10 * 1024 * 1024),
+        cost_estimate=pl.CostEstimate(flops=300_000_000, bytes_accessed=4_000_000, transcendentals=0),
+    )(*[pltpu.with_memory_space_constraint(a, pltpu.HBM) for a in held])
     codes_in = lax.all_to_all(sent, SPREAD, 0, 0, tiled=True)
 
     built = call(
         build_kernel, jax.ShapeDtypeStruct((blocks, row_lines + 8, LANES), BF16), 1_200_000_000, 8_000_000
-    )(codes_in, decoder)
+    )(codes_in, weights)
     rows_in = lax.all_to_all(built, PLANE, 0, 0, tiled=True)
     partial, hot = call(
         reduce_kernel,
@@ -284,12 +312,11 @@
         ),
         1_300_000_000,
         8_000_000,
-    )(grad_in, codes_in, decoder)
+    )(grad_in, codes_in, weights)
     scores_in = lax.all_to_all(scored, SPREAD, 0, 0, tiled=True)
-    placed = call(place_kernel, jax.ShapeDtypeStruct((layers, rows, panel), BF16), 140_000_000, 1_000_000)(
+    scores = call(place_kernel, jax.ShapeDtypeStruct(feature_codes.shape, BF16), 140_000_000, 1_000_000)(
         slot, scores_in
     )
-    scores = placed.reshape(layers, kact, count, panel).transpose(0, 2, 1, 3)
     return scores, totals
 
 

time: 231 us -> 229 us (level)
  local copies, waits for them, and re-layouts: 3.63 us -> 0.01 us
where the time goes in v4:
time: 229 us; the launch traced here: 228 us
  blocking collectives  218 us (95%)
  Pallas kernels  9.12 us (4%)
    all_to_all x1, blocking collectives, per_device(): rows_in = lax.all_to_all(built, PLANE, 0, 0, tiled=True)  64.2 us
    all_to_all x1, blocking collectives, per_device(): grad_in = lax.all_to_all(spread, PLANE, 0, 0, tiled=True)  63 us
    all_to_all x1, blocking collectives, per_device(): codes_in = lax.all_to_all(sent, SPREAD, 0, 0, tiled=True)  31.4 us
    all_to_all x1, blocking collectives, per_device(): scores_in = lax.all_to_all(scored, SPREAD, 0, 0, tiled=True)  20.3 us
    all_to_all x1, blocking collectives, per_device(): lax.all_to_all(copies, COLUMN, 0, 0, tiled=True).reshape(count, width)  19.9 us
    all_to_all x1, blocking collectives, per_device(): lax.all_to_all(partial.reshape(planes, share, width), COLUMN, 0, 0, tiled...  19.3 us

profile of v4, /device:TPU:1, one launch (start us, length us, event | category | flops | bytes accessed | tf_op | source)
XLA Modules:
  0.0 227.9 jit_solution(8381644248183279869)
XLA Ops:
  0.6 1.8 shard_map.77
  2.5 31.4 %all_to_all.30.codes_ref = bf16[32,72,128]{2,1,0:T(8,128)(2,1)S(1)} all-to-all(bf16[32,72,128]{2,1,0:T(8,128)(2,1)S(1)} %get-tuple-element.10), channel_id=1, replica_groups=mesh['zh'=4,'x'=4,'c'=2,'zl'=2,'y'=4] {'x','zh','c'}, dimensions={0} | all-to-all | bytes 1179648 | tf_op jit(solution)/shard_map/all_to_all | solution.py:286
  33.9 1.4 shard_map.78
  35.3 0.0 copy-start
  35.3 64.2 %all_to_all.31.rows_ref = bf16[32,584,128]{2,1,0:T(8,128)(2,1)S(1)} all-to-all(bf16[32,584,128]{2,1,0:T(8,128)(2,1)S(1)} %shard_map.78), channel_id=1, replica_groups=mesh['zh'=4,'x'=4,'c'=2,'zl'=2,'y'=4] {'x','y','c'}, dimensions={0} | all-to-all | bytes 9568256 | tf_op jit(solution)/shard_map/all_to_all | solution.py:291
  99.5 0.0 copy-done
  99.5 0.8 shard_map.79
  100.3 19.3 %all_to_all.32.parts_ref = bf16[8,16,2304]{2,1,0:T(8,128)(2,1)S(1)} all-to-all(bf16[8,16,2304]{2,1,0:T(8,128)(2,1)S(1)} %bitcast.6), channel_id=1, replica_groups=mesh['zh'=4,'x'=4,'c'=2,'zl'=2,'y'=4] {'zl','zh'}, dimensions={0} | all-to-all | bytes 1179648 | tf_op jit(solution)/shard_map/all_to_all | solution.py:298
  119.7 0.2 shard_map.80
  119.9 19.9 %all_to_all.33 = bf16[8,16,2304]{2,1,0:T(8,128)(2,1)S(1)} all-to-all(bf16[8,16,2304]{2,1,0:T(8,128)(2,1)S(1)} %shard_map.80), channel_id=1, replica_groups=mesh['zh'=4,'x'=4,'c'=2,'zl'=2,'y'=4] {'zl','zh'}, dimensions={0} | all-to-all | bytes 1179648 | tf_op jit(solution)/shard_map/all_to_all | solution.py:302
  139.7 1.4 shard_map.81
  141.1 63.0 %all_to_all.34.rows_ref = bf16[32,576,128]{2,1,0:T(8,128)(2,1)S(1)} all-to-all(bf16[32,576,128]{2,1,0:T(8,128)(2,1)S(1)} %shard_map.81), channel_id=1, replica_groups=mesh['zh'=4,'x'=4,'c'=2,'zl'=2,'y'=4] {'x','y','c'}, dimensions={0} | all-to-all | bytes 9437184 | tf_op jit(solution)/shard_map/all_to_all | solution.py:306
  204.1 2.4 %shard_map.82 = (bf16[32,64,128]{2,1,0:T(8,128)(2,1)S(1)}, f32[16,2,256]{2,1,0:T(2,128)}) custom-call(bf16[32,576,128]{2,1,0:T(8,128)(2,1)S(1)} %all_to_all.34.rows_ref, bf16[32,72,128]{2,1,0:T(8,128)(2,1)S(1)} %all_to_all.30.codes_ref, bf16[2,256,2304]{2,1,0:T(8,128)(2,1)S(1)} %get-tuple-element.11.weight_ref), custom_call_target="tpu_custom_call" | custom-call | flops 1300000000 | bytes 8000000 | tf_op jit(solution)/shard_map/pallas_call | solution.py:307
  206.5 20.3 %all_to_all.35.scores_ref = bf16[32,64,128]{2,1,0:T(8,128)(2,1)S(1)} all-to-all(bf16[32,64,128]{2,1,0:T(8,128)(2,1)S(1)} %get-tuple-element.14), channel_id=1, replica_groups=mesh['zh'=4,'x'=4,'c'=2,'zl'=2,'y'=4] {'x','zh','c'}, dimensions={0} | all-to-all | bytes 1048576 | tf_op jit(solution)/shard_map/all_to_all | solution.py:316
  226.8 1.1 shard_map.83
Async XLA Ops:
  35.3 64.2 %copy-start = (bf16[128,2304]{1,0:T(8,128)(2,1)S(1)}, bf16[128,2304]{1,0:T(8,128)(2,1)}, u32[]{:S(2)}) copy-start(bf16[128,2304]{1,0:T(8,128)(2,1)} %resid_ref.1) | copy-start | bytes 1769476

commit v5 on v4

--- a/solution.py
+++ b/solution.py
@@ -10,9 +10,9 @@
 CAP = 16
 LANES = 128
 TOK = ("zh", "x", "c")
-SPREAD = ("x", "zh", "c")
+SPREAD = ("x", "c", "zh")
 LYR = ("zl", "y")
-PLANE = ("x", "y", "c")
+PLANE = ("x", "c", "y")
 COLUMN = ("zl", "zh")
 EVERY = ("zh", "x", "c", "zl", "y")
 BF16 = jnp.bfloat16
@@ -84,7 +84,7 @@
     for l in range(layers):
         panel_id = sum(spaced[k][l * kact + k : l * kact + k + 1] for k in range(kact)).astype(jnp.int32)
         zh, x, c = panel_id // 8, panel_id // 2 % 4, panel_id % 2
-        ids_row = (x * 8 + zh * 2 + c).astype(F32)
+        ids_row = (x * 8 + c * 4 + zh).astype(F32)
         ids_col = to_column(ids_row)
         earlier = (ids_col == ids_row) & (iota((rows, rows), 0) < iota((rows, rows), 1))
         rank = jnp.sum(jnp.where(earlier, 1.0, 0.0), axis=0, keepdims=True)
@@ -102,8 +102,7 @@
         token_info += jnp.dot(jnp.where(named, token_row, 0.0).astype(BF16), place, preferred_element_type=F32)
         request_info += jnp.dot(jnp.where(named, request_row, 0.0).astype(BF16), place, preferred_element_type=F32)
     spot = iota((PANELS, LANES), 1) // slots
-    sender = lax.axis_index("y") % 2 * 2 + iota((PANELS, LANES), 0) % 2
-    token_info = jnp.where(spot == sender, token_info, 0.0)
+    token_info = jnp.where(spot == lax.axis_index("y") % per, token_info, 0.0)
     request_info = jnp.where(spot == lax.axis_index(SPREAD) % per, request_info, 0.0)
     line = iota((PANELS, 8, LANES), 1)
     tile = jnp.where(

time: 229 us -> 228 us (level)
  no operation moved by 1% of the time
where the time goes in v5:
time: 228 us
  blocking collectives  218 us (96%)
  Pallas kernels  9.12 us (4%)
    all_to_all x1, blocking collectives, per_device(): grad_in = lax.all_to_all(spread, PLANE, 0, 0, tiled=True)  64.9 us
    all_to_all x1, blocking collectives, per_device(): rows_in = lax.all_to_all(built, PLANE, 0, 0, tiled=True)  63.7 us
    all_to_all x1, blocking collectives, per_device(): codes_in = lax.all_to_all(sent, SPREAD, 0, 0, tiled=True)  31.6 us
    all_to_all x1, blocking collectives, per_device(): scores_in = lax.all_to_all(scored, SPREAD, 0, 0, tiled=True)  21.3 us
    all_to_all x1, blocking collectives, per_device(): lax.all_to_all(partial.reshape(planes, share, width), COLUMN, 0, 0, tiled...  18.7 us
    all_to_all x1, blocking collectives, per_device(): lax.all_to_all(copies, COLUMN, 0, 0, tiled=True).reshape(count, width)  18 us

profile of v5, /device:TPU:1, one launch (start us, length us, event | category | flops | bytes accessed | tf_op | source)
XLA Modules:
  0.0 228.1 jit_solution(3599195186977369018)
XLA Ops:
  0.6 1.8 shard_map.77
  2.5 31.6 %all_to_all.30.codes_ref = bf16[32,72,128]{2,1,0:T(8,128)(2,1)S(1)} all-to-all(bf16[32,72,128]{2,1,0:T(8,128)(2,1)S(1)} %get-tuple-element.10), channel_id=1, replica_groups=mesh['zh'=4,'x'=4,'c'=2,'zl'=2,'y'=4] {'x','c','zh'}, dimensions={0} | all-to-all | bytes 1179648 | tf_op jit(solution)/shard_map/all_to_all | solution.py:285
  34.1 1.4 shard_map.78
  35.5 0.0 copy-start
  35.5 63.7 %all_to_all.31.rows_ref = bf16[32,584,128]{2,1,0:T(8,128)(2,1)S(1)} all-to-all(bf16[32,584,128]{2,1,0:T(8,128)(2,1)S(1)} %shard_map.78), channel_id=1, replica_groups=mesh['zh'=4,'x'=4,'c'=2,'zl'=2,'y'=4] {'x','c','y'}, dimensions={0} | all-to-all | bytes 9568256 | tf_op jit(solution)/shard_map/all_to_all | solution.py:290
  99.2 0.0 copy-done
  99.2 0.8 shard_map.79
  100.0 18.7 %all_to_all.32.parts_ref = bf16[8,16,2304]{2,1,0:T(8,128)(2,1)S(1)} all-to-all(bf16[8,16,2304]{2,1,0:T(8,128)(2,1)S(1)} %bitcast.6), channel_id=1, replica_groups=mesh['zh'=4,'x'=4,'c'=2,'zl'=2,'y'=4] {'zl','zh'}, dimensions={0} | all-to-all | bytes 1179648 | tf_op jit(solution)/shard_map/all_to_all | solution.py:297
  118.7 0.2 shard_map.80
  118.9 18.0 %all_to_all.33 = bf16[8,16,2304]{2,1,0:T(8,128)(2,1)S(1)} all-to-all(bf16[8,16,2304]{2,1,0:T(8,128)(2,1)S(1)} %shard_map.80), channel_id=1, replica_groups=mesh['zh'=4,'x'=4,'c'=2,'zl'=2,'y'=4] {'zl','zh'}, dimensions={0} | all-to-all | bytes 1179648 | tf_op jit(solution)/shard_map/all_to_all | solution.py:301
  136.9 1.4 shard_map.81
  138.3 64.9 %all_to_all.34.rows_ref = bf16[32,576,128]{2,1,0:T(8,128)(2,1)S(1)} all-to-all(bf16[32,576,128]{2,1,0:T(8,128)(2,1)S(1)} %shard_map.81), channel_id=1, replica_groups=mesh['zh'=4,'x'=4,'c'=2,'zl'=2,'y'=4] {'x','c','y'}, dimensions={0} | all-to-all | bytes 9437184 | tf_op jit(solution)/shard_map/all_to_all | solution.py:305
  203.2 2.4 %shard_map.82 = (bf16[32,64,128]{2,1,0:T(8,128)(2,1)S(1)}, f32[16,2,256]{2,1,0:T(2,128)}) custom-call(bf16[32,576,128]{2,1,0:T(8,128)(2,1)S(1)} %all_to_all.34.rows_ref, bf16[32,72,128]{2,1,0:T(8,128)(2,1)S(1)} %all_to_all.30.codes_ref, bf16[2,256,2304]{2,1,0:T(8,128)(2,1)S(1)} %get-tuple-element.11.weight_ref), custom_call_target="tpu_custom_call" | custom-call | flops 1300000000 | bytes 8000000 | tf_op jit(solution)/shard_map/pallas_call | solution.py:306
  205.6 21.3 %all_to_all.35.scores_ref = bf16[32,64,128]{2,1,0:T(8,128)(2,1)S(1)} all-to-all(bf16[32,64,128]{2,1,0:T(8,128)(2,1)S(1)} %get-tuple-element.14), channel_id=1, replica_groups=mesh['zh'=4,'x'=4,'c'=2,'zl'=2,'y'=4] {'x','c','zh'}, dimensions={0} | all-to-all | bytes 1048576 | tf_op jit(solution)/shard_map/all_to_all | solution.py:315
  226.9 1.1 shard_map.83
Async XLA Ops:
  35.5 63.7 %copy-start = (bf16[128,2304]{1,0:T(8,128)(2,1)S(1)}, bf16[128,2304]{1,0:T(8,128)(2,1)}, u32[]{:S(2)}) copy-start(bf16[128,2304]{1,0:T(8,128)(2,1)} %resid_ref.1) | copy-start | bytes 1769476

commit v6 on v5

--- a/solution.py
+++ b/solution.py
@@ -188,7 +188,7 @@
             out_ref[:, at : at + slots, :] = rows[:, i : i + LANES].reshape(groups, slots, LANES)
 
 
-def project_kernel(rows_ref, codes_ref, weight_ref, score_ref, total_ref):
+def project_kernel(rows_ref, codes_ref, weight_ref, score_ref, rest_ref):
     blocks = rows_ref.shape[0]
     layers, panel, width = weight_ref.shape
     slots = layers * CAP
@@ -205,6 +205,24 @@
         projections.append(
             lax.dot_general(rows, weight_ref[l], (((1,), (1,)), ((), ())), preferred_element_type=F32).astype(BF16)
         )
+    for h in range(halves):
+        for l in range(layers):
+            at = slice(h * slots + l * CAP, h * slots + (l + 1) * CAP)
+            codes = codes_ref[:, at, :].reshape(blocks * CAP, LANES).astype(F32)
+            projected = projections[l][:, h * LANES : (h + 1) * LANES].astype(F32)
+            value = codes * projected
+            upper = value.astype(BF16)
+            score_ref[:, at, :] = upper.reshape(blocks, CAP, LANES)
+            rest_ref[:, at, :] = (value - upper.astype(F32)).astype(BF16).reshape(blocks, CAP, LANES)
+
+
+def place_kernel(
+    slot_ref, scores_ref, codes_ref, upper_ref, rest_ref, out_hbm, total_hbm, out_ref, total_ref, sems
+):
+    layers, rows = slot_ref.shape
+    blocks = codes_ref.shape[0]
+    slots = layers * CAP
+    halves = out_ref.shape[3] // LANES
     request = lane_groups(codes_ref[:, halves * slots : halves * slots + 8, :].astype(F32)[:, 1:2, :])
     lane_layer = iota((layers * REQUESTS, LANES), 1) % slots // CAP
     line = iota((layers * REQUESTS, LANES), 0)
@@ -214,28 +232,14 @@
         [jnp.where((request[g] == want) & here, 1.0, 0.0) for g in range(blocks * slots // LANES)], axis=1
     ).astype(BF16)
     for h in range(halves):
-        values = []
-        for l in range(layers):
-            at = slice(h * slots + l * CAP, h * slots + (l + 1) * CAP)
-            codes = codes_ref[:, at, :].reshape(blocks * CAP, LANES).astype(F32)
-            projected = projections[l][:, h * LANES : (h + 1) * LANES].astype(F32)
-            value = codes * projected
-            score_ref[:, at, :] = value.astype(BF16).reshape(blocks, CAP, LANES)
-            values.append(value.reshape(blocks, CAP, LANES))
-        value = jnp.concatenate(values, axis=1).reshape(blocks * slots, LANES)
-        upper = value.astype(BF16)
-        lower = (value - upper.astype(F32)).astype(BF16)
-        summed = jnp.dot(member, upper, preferred_element_type=F32) + jnp.dot(
-            member, lower, preferred_element_type=F32
-        )
+        lines = slice(h * slots, (h + 1) * slots)
+        summed = jnp.dot(
+            member, upper_ref[:, lines, :].reshape(blocks * slots, LANES), preferred_element_type=F32
+        ) + jnp.dot(member, rest_ref[:, lines, :].reshape(blocks * slots, LANES), preferred_element_type=F32)
         for l in range(layers):
             total_ref[:, l, h * LANES : (h + 1) * LANES] = summed[l * REQUESTS : (l + 1) * REQUESTS]
-
-
-def place_kernel(slot_ref, scores_ref, out_ref):
-    layers, rows = slot_ref.shape
-    slots = layers * CAP
-    halves = out_ref.shape[3] // LANES
+    copies = [pltpu.make_async_copy(total_ref, total_hbm, sems.at[layers])]
+    copies[0].start()
     for l in range(layers):
         column = to_column(slot_ref[l : l + 1, :])
         pick = jnp.where(iota((rows, PANELS * CAP), 1) == column, 1.0, 0.0).astype(BF16)
@@ -248,6 +252,10 @@
         )
         placed = jnp.dot(pick, scores, preferred_element_type=F32).astype(BF16)
         out_ref[l] = placed.reshape(out_ref.shape[1:])
+        copies.append(pltpu.make_async_copy(out_ref.at[l], out_hbm.at[l], sems.at[l]))
+        copies[-1].start()
+    for copy in copies:
+        copy.wait()
 
 
 def per_device(feature_codes, block_ids, target_layer, request_ids, target_resid, decoder):
@@ -303,20 +311,25 @@
         hot, gradient
     )
     grad_in = lax.all_to_all(spread, PLANE, 0, 0, tiled=True)
-    scored, totals = call(
-        project_kernel,
-        (
-            jax.ShapeDtypeStruct((blocks, code_lines, LANES), BF16),
+    piece = jax.ShapeDtypeStruct((blocks, code_lines, LANES), BF16)
+    scored, rest = call(project_kernel, (piece, piece), 1_300_000_000, 8_000_000)(grad_in, codes_in, weights)
+    scores_in = lax.all_to_all(scored, SPREAD, 0, 0, tiled=True)
+    anywhere = pl.BlockSpec(memory_space=pl.ANY)
+    return pl.pallas_call(
+        place_kernel,
+        out_shape=(
+            jax.ShapeDtypeStruct(feature_codes.shape, BF16),
             jax.ShapeDtypeStruct((REQUESTS, layers, panel), F32),
         ),
-        1_300_000_000,
-        8_000_000,
-    )(grad_in, codes_in, weights)
-    scores_in = lax.all_to_all(scored, SPREAD, 0, 0, tiled=True)
-    scores = call(place_kernel, jax.ShapeDtypeStruct(feature_codes.shape, BF16), 140_000_000, 1_000_000)(
-        slot, scores_in
-    )
-    return scores, totals
+        out_specs=(anywhere, anywhere),
+        scratch_shapes=[
+            pltpu.VMEM(feature_codes.shape, BF16),
+            pltpu.VMEM((REQUESTS, layers, panel), F32),
+            pltpu.SemaphoreType.DMA((layers + 1,)),
+        ],
+        compiler_params=pltpu.CompilerParams(vmem_limit_bytes=10 * 1024 * 1024),
+        cost_estimate=pl.CostEstimate(flops=270_000_000, bytes_accessed=2_000_000, transcendentals=0),
+    )(slot, scores_in, codes_in, scored, rest)
 
 
 def solution(mesh):

time: 228 us -> 228 us (level)
  no operation moved by 1% of the time
where the time goes in v6:
time: 228 us; the launch traced here: 227 us
  blocking collectives  218 us (96%)
  Pallas kernels  8.35 us (4%)
    all_to_all x1, blocking collectives, per_device(): grad_in = lax.all_to_all(spread, PLANE, 0, 0, tiled=True)  64.9 us
    all_to_all x1, blocking collectives, per_device(): rows_in = lax.all_to_all(built, PLANE, 0, 0, tiled=True)  63.7 us
    all_to_all x1, blocking collectives, per_device(): codes_in = lax.all_to_all(sent, SPREAD, 0, 0, tiled=True)  31.6 us
    all_to_all x1, blocking collectives, per_device(): scores_in = lax.all_to_all(scored, SPREAD, 0, 0, tiled=True)  21.3 us
    all_to_all x1, blocking collectives, per_device(): lax.all_to_all(partial.reshape(planes, share, width), COLUMN, 0, 0, tiled...  18.7 us
    all_to_all x1, blocking collectives, per_device(): lax.all_to_all(copies, COLUMN, 0, 0, tiled=True).reshape(count, width)  18 us

profile of v6, /device:TPU:1, one launch (start us, length us, event | category | flops | bytes accessed | tf_op | source)
XLA Modules:
  0.0 227.3 jit_solution(3938867876269647048)
XLA Ops:
  0.6 1.8 shard_map.77
  2.5 31.6 %all_to_all.30.codes_ref = bf16[32,72,128]{2,1,0:T(8,128)(2,1)S(1)} all-to-all(bf16[32,72,128]{2,1,0:T(8,128)(2,1)S(1)} %get-tuple-element.10), channel_id=1, replica_groups=mesh['zh'=4,'x'=4,'c'=2,'zl'=2,'y'=4] {'x','c','zh'}, dimensions={0} | all-to-all | bytes 1179648 | tf_op jit(solution)/shard_map/all_to_all | solution.py:293
  34.1 1.4 shard_map.78
  35.5 0.0 copy-start
  35.5 63.7 %all_to_all.31.rows_ref = bf16[32,584,128]{2,1,0:T(8,128)(2,1)S(1)} all-to-all(bf16[32,584,128]{2,1,0:T(8,128)(2,1)S(1)} %shard_map.78), channel_id=1, replica_groups=mesh['zh'=4,'x'=4,'c'=2,'zl'=2,'y'=4] {'x','c','y'}, dimensions={0} | all-to-all | bytes 9568256 | tf_op jit(solution)/shard_map/all_to_all | solution.py:298
  99.2 0.0 copy-done
  99.2 0.8 shard_map.79
  100.0 18.7 %all_to_all.32.parts_ref = bf16[8,16,2304]{2,1,0:T(8,128)(2,1)S(1)} all-to-all(bf16[8,16,2304]{2,1,0:T(8,128)(2,1)S(1)} %bitcast.6), channel_id=1, replica_groups=mesh['zh'=4,'x'=4,'c'=2,'zl'=2,'y'=4] {'zl','zh'}, dimensions={0} | all-to-all | bytes 1179648 | tf_op jit(solution)/shard_map/all_to_all | solution.py:305
  118.7 0.2 shard_map.80
  118.9 18.0 %all_to_all.33 = bf16[8,16,2304]{2,1,0:T(8,128)(2,1)S(1)} all-to-all(bf16[8,16,2304]{2,1,0:T(8,128)(2,1)S(1)} %shard_map.80), channel_id=1, replica_groups=mesh['zh'=4,'x'=4,'c'=2,'zl'=2,'y'=4] {'zl','zh'}, dimensions={0} | all-to-all | bytes 1179648 | tf_op jit(solution)/shard_map/all_to_all | solution.py:309
  136.9 1.4 shard_map.81
  138.3 64.9 %all_to_all.34.rows_ref = bf16[32,576,128]{2,1,0:T(8,128)(2,1)S(1)} all-to-all(bf16[32,576,128]{2,1,0:T(8,128)(2,1)S(1)} %shard_map.81), channel_id=1, replica_groups=mesh['zh'=4,'x'=4,'c'=2,'zl'=2,'y'=4] {'x','c','y'}, dimensions={0} | all-to-all | bytes 9437184 | tf_op jit(solution)/shard_map/all_to_all | solution.py:313
  203.2 1.5 shard_map.82
  204.7 21.3 %all_to_all.35.scores_ref = bf16[32,64,128]{2,1,0:T(8,128)(2,1)S(1)} all-to-all(bf16[32,64,128]{2,1,0:T(8,128)(2,1)S(1)} %get-tuple-element.14.upper_ref), channel_id=1, replica_groups=mesh['zh'=4,'x'=4,'c'=2,'zl'=2,'y'=4] {'x','c','zh'}, dimensions={0} | all-to-all | bytes 1048576 | tf_op jit(solution)/shard_map/all_to_all | solution.py:316
  226.1 1.2 shard_map.83
Async XLA Ops:
  35.5 63.7 %copy-start = (bf16[128,2304]{1,0:T(8,128)(2,1)S(1)}, bf16[128,2304]{1,0:T(8,128)(2,1)}, u32[]{:S(2)}) copy-start(bf16[128,2304]{1,0:T(8,128)(2,1)} %resid_ref.1) | copy-start | bytes 1769476

commit v7 on v6

--- a/solution.py
+++ b/solution.py
@@ -51,7 +51,7 @@
 ):
     pairs = (
         (ids_hbm, ids_ref), (target_hbm, target_ref), (request_hbm, request_ref), (codes_hbm, codes_ref),
-        (weight_hbm, weight_out),
+        (weight_hbm.at[0], weight_out),
     )
     loads = [pltpu.make_async_copy(source, held, sems.at[i]) for i, (source, held) in enumerate(pairs)]
     for load in loads:
@@ -114,9 +114,11 @@
     loads[-1].wait()
 
 
-def build_kernel(codes_ref, weight_ref, out_ref):
+def build_kernel(codes_ref, first_ref, weight_hbm, out_ref, rest_ref, rest_sem):
+    load = pltpu.make_async_copy(weight_hbm.at[1:], rest_ref, rest_sem)
+    load.start()
     blocks = codes_ref.shape[0]
-    layers, panel, width = weight_ref.shape
+    layers, panel, width = weight_hbm.shape
     slots = layers * CAP
     halves = panel // LANES
     step = 2 * LANES
@@ -128,8 +130,11 @@
             ],
             axis=1,
         )
+        if l == 1:
+            load.wait()
         for n in range(0, width, step):
-            built = jnp.dot(codes, weight_ref[l, :, n : n + step], preferred_element_type=F32).astype(BF16)
+            weight = first_ref[:, n : n + step] if l == 0 else rest_ref[l - 1, :, n : n + step]
+            built = jnp.dot(codes, weight, preferred_element_type=F32).astype(BF16)
             for i in range(0, step, LANES):
                 at = (n + i) // LANES * slots + l * CAP
                 out_ref[:, at : at + CAP, :] = built[:, i : i + LANES].reshape(blocks, CAP, LANES)
@@ -188,9 +193,10 @@
             out_ref[:, at : at + slots, :] = rows[:, i : i + LANES].reshape(groups, slots, LANES)
 
 
-def project_kernel(rows_ref, codes_ref, weight_ref, score_ref, rest_ref):
+def project_kernel(rows_ref, codes_ref, first_ref, weights_ref, score_ref, rest_ref):
     blocks = rows_ref.shape[0]
-    layers, panel, width = weight_ref.shape
+    panel, width = first_ref.shape
+    layers = weights_ref.shape[0] + 1
     slots = layers * CAP
     halves = panel // LANES
     projections = []
@@ -203,7 +209,7 @@
             axis=1,
         )
         projections.append(
-            lax.dot_general(rows, weight_ref[l], (((1,), (1,)), ((), ())), preferred_element_type=F32).astype(BF16)
+            lax.dot_general(rows, first_ref[...] if l == 0 else weights_ref[l - 1], (((1,), (1,)), ((), ())), preferred_element_type=F32).astype(BF16)
         )
     for h in range(halves):
         for l in range(layers):
@@ -277,12 +283,12 @@
         feature_codes,
         decoder,
     )
-    sent, slot, weights = pl.pallas_call(
+    sent, slot, first = pl.pallas_call(
         pack_kernel,
         out_shape=(
             jax.ShapeDtypeStruct((blocks, code_lines + 8, LANES), BF16),
             jax.ShapeDtypeStruct((layers, rows), jnp.int32),
-            jax.ShapeDtypeStruct(decoder.shape, decoder.dtype),
+            jax.ShapeDtypeStruct(decoder.shape[1:], decoder.dtype),
         ),
         in_specs=[offchip] * len(held),
         out_specs=(onchip, onchip, pl.BlockSpec(memory_space=pl.ANY)),
@@ -292,9 +298,18 @@
     )(*[pltpu.with_memory_space_constraint(a, pltpu.HBM) for a in held])
     codes_in = lax.all_to_all(sent, SPREAD, 0, 0, tiled=True)
 
-    built = call(
-        build_kernel, jax.ShapeDtypeStruct((blocks, row_lines + 8, LANES), BF16), 1_200_000_000, 8_000_000
-    )(codes_in, weights)
+    built, rest_weights = pl.pallas_call(
+        build_kernel,
+        out_shape=(
+            jax.ShapeDtypeStruct((blocks, row_lines + 8, LANES), BF16),
+            jax.ShapeDtypeStruct((layers - 1,) + decoder.shape[1:], decoder.dtype),
+        ),
+        in_specs=[onchip, onchip, offchip],
+        out_specs=(onchip, pl.BlockSpec(memory_space=pltpu.VMEM)),
+        scratch_shapes=[pltpu.SemaphoreType.DMA],
+        compiler_params=pltpu.CompilerParams(vmem_limit_bytes=10 * 1024 * 1024),
+        cost_estimate=pl.CostEstimate(flops=1_200_000_000, bytes_accessed=8_000_000, transcendentals=0),
+    )(codes_in, first, pltpu.with_memory_space_constraint(decoder, pltpu.HBM))
     rows_in = lax.all_to_all(built, PLANE, 0, 0, tiled=True)
     partial, hot = call(
         reduce_kernel,
@@ -312,7 +327,9 @@
     )
     grad_in = lax.all_to_all(spread, PLANE, 0, 0, tiled=True)
     piece = jax.ShapeDtypeStruct((blocks, code_lines, LANES), BF16)
-    scored, rest = call(project_kernel, (piece, piece), 1_300_000_000, 8_000_000)(grad_in, codes_in, weights)
+    scored, rest = call(project_kernel, (piece, piece), 1_300_000_000, 8_000_000)(
+        grad_in, codes_in, first, rest_weights
+    )
     scores_in = lax.all_to_all(scored, SPREAD, 0, 0, tiled=True)
     anywhere = pl.BlockSpec(memory_space=pl.ANY)
     return pl.pallas_call(

time: 228 us -> 228 us (level)
  no operation moved by 1% of the time
where the time goes in v7:
time: 228 us
  blocking collectives  218 us (96%)
  Pallas kernels  8.83 us (4%)
    all_to_all x1, blocking collectives, per_device(): grad_in = lax.all_to_all(spread, PLANE, 0, 0, tiled=True)  64.9 us
    all_to_all x1, blocking collectives, per_device(): rows_in = lax.all_to_all(built, PLANE, 0, 0, tiled=True)  63.7 us
    all_to_all x1, blocking collectives, per_device(): codes_in = lax.all_to_all(sent, SPREAD, 0, 0, tiled=True)  31.6 us
    all_to_all x1, blocking collectives, per_device(): scores_in = lax.all_to_all(scored, SPREAD, 0, 0, tiled=True)  21.3 us
    all_to_all x1, blocking collectives, per_device(): lax.all_to_all(partial.reshape(planes, share, width), COLUMN, 0, 0, tiled...  18.7 us
    all_to_all x1, blocking collectives, per_device(): lax.all_to_all(copies, COLUMN, 0, 0, tiled=True).reshape(count, width)  18 us

profile of v7, /device:TPU:1, one launch (start us, length us, event | category | flops | bytes accessed | tf_op | source)
XLA Modules:
  0.0 227.8 jit_solution(1771267021117549874)
XLA Ops:
  0.6 1.6 shard_map.77
  2.2 31.6 %all_to_all.30.codes_ref = bf16[32,72,128]{2,1,0:T(8,128)(2,1)S(1)} all-to-all(bf16[32,72,128]{2,1,0:T(8,128)(2,1)S(1)} %get-tuple-element.12), channel_id=1, replica_groups=mesh['zh'=4,'x'=4,'c'=2,'zl'=2,'y'=4] {'x','c','zh'}, dimensions={0} | all-to-all | bytes 1179648 | tf_op jit(solution)/shard_map/all_to_all | solution.py:299
  33.8 2.1 shard_map.78
  35.9 0.0 copy-start
  36.0 63.7 %all_to_all.31.rows_ref = bf16[32,584,128]{2,1,0:T(8,128)(2,1)S(1)} all-to-all(bf16[32,584,128]{2,1,0:T(8,128)(2,1)S(1)} %get-tuple-element.14), channel_id=1, replica_groups=mesh['zh'=4,'x'=4,'c'=2,'zl'=2,'y'=4] {'x','c','y'}, dimensions={0} | all-to-all | bytes 9568256 | tf_op jit(solution)/shard_map/all_to_all | solution.py:313
  99.6 0.0 copy-done
  99.6 0.8 shard_map.79
  100.4 18.7 %all_to_all.32.parts_ref = bf16[8,16,2304]{2,1,0:T(8,128)(2,1)S(1)} all-to-all(bf16[8,16,2304]{2,1,0:T(8,128)(2,1)S(1)} %bitcast.6), channel_id=1, replica_groups=mesh['zh'=4,'x'=4,'c'=2,'zl'=2,'y'=4] {'zl','zh'}, dimensions={0} | all-to-all | bytes 1179648 | tf_op jit(solution)/shard_map/all_to_all | solution.py:320
  119.2 0.2 shard_map.80
  119.4 18.0 %all_to_all.33 = bf16[8,16,2304]{2,1,0:T(8,128)(2,1)S(1)} all-to-all(bf16[8,16,2304]{2,1,0:T(8,128)(2,1)S(1)} %shard_map.80), channel_id=1, replica_groups=mesh['zh'=4,'x'=4,'c'=2,'zl'=2,'y'=4] {'zl','zh'}, dimensions={0} | all-to-all | bytes 1179648 | tf_op jit(solution)/shard_map/all_to_all | solution.py:324
  137.4 1.4 shard_map.81
  138.7 64.9 %all_to_all.34.rows_ref = bf16[32,576,128]{2,1,0:T(8,128)(2,1)S(1)} all-to-all(bf16[32,576,128]{2,1,0:T(8,128)(2,1)S(1)} %shard_map.81), channel_id=1, replica_groups=mesh['zh'=4,'x'=4,'c'=2,'zl'=2,'y'=4] {'x','c','y'}, dimensions={0} | all-to-all | bytes 9437184 | tf_op jit(solution)/shard_map/all_to_all | solution.py:328
  203.7 1.5 shard_map.82
  205.2 21.3 %all_to_all.35.scores_ref = bf16[32,64,128]{2,1,0:T(8,128)(2,1)S(1)} all-to-all(bf16[32,64,128]{2,1,0:T(8,128)(2,1)S(1)} %get-tuple-element.18.upper_ref), channel_id=1, replica_groups=mesh['zh'=4,'x'=4,'c'=2,'zl'=2,'y'=4] {'x','c','zh'}, dimensions={0} | all-to-all | bytes 1048576 | tf_op jit(solution)/shard_map/all_to_all | solution.py:333
  226.5 1.2 shard_map.83
Async XLA Ops:
  35.9 63.7 %copy-start = (bf16[128,2304]{1,0:T(8,128)(2,1)S(1)}, bf16[128,2304]{1,0:T(8,128)(2,1)}, u32[]{:S(2)}) copy-start(bf16[128,2304]{1,0:T(8,128)(2,1)} %resid_ref.1) | copy-start | bytes 1769476
